TPU v7x, 256 devices: a whole 4x4x8 slice. The times are simulated.
256 devices in a mesh: wide: 32 (over x, y, core), narrow: 8 (over z).
Axes of the slice: x: 4, y: 4, z: 8, core: 2. Of those that a mesh axis runs over, the one named last changes fastest.
Arguments:
- corpus: float32 [524288, 1024], P(('wide', 'narrow')), may hold values from -30 to 30
- sketch: float32 [1024, 256], replicated, may hold values from -0.125 to 0.125
Outputs:
- basis: float32 [524288, 256], P(('wide', 'narrow'))
- projection: float32 [256, 1024], replicated
All inputs are finite; a program needn't handle non-finite values.
Results may differ from a plain program's by a relative error of at most 0.0003.
Values sent between devices are 32-bit elements; how exact they have to be, the bound alone decides.
No kernel may reach another device: no remote copies, remote signals or barrier semaphores. Data moves between devices by JAX's collectives and lax.ppermute only.
A program may use at most 64 MiB of HBM per device.

v0:
```python
import math

import jax
import jax.numpy as jnp
from jax import lax
from jax.experimental import pallas as pl
from jax.experimental.pallas import tpu as pltpu
from jax.sharding import Mesh
from jax.sharding import PartitionSpec as P

WIDE_NARROW = ("wide_0", "wide_1", "wide_2", "narrow")
PLANE = ("wide_0", "wide_1")
CORE = "wide_2"
LINE = "narrow"
HI = lax.Precision.HIGHEST
F32 = jnp.float32
BF16 = jnp.bfloat16
ROWS_PER_STEP = 512
BLOCK = 64


def dot(a, b, dims=((1,), (0,)), precision=HI):
    return lax.dot_general(a, b, (dims, ((), ())), precision=precision, preferred_element_type=F32)


def dot16(a, b, dims=((1,), (0,))):
    return lax.dot_general(a, b, (dims, ((), ())), preferred_element_type=F32)


def split3(x):
    a = x.astype(BF16)
    r = x - a.astype(F32)
    b = r.astype(BF16)
    return a, b, (r - b.astype(F32)).astype(BF16)


def two_sum(a, b):
    s = a + b
    t = s - a
    return s, (a - (s - t)) + (b - t)


def grid_slices(x, top):
    out = []
    for i in range(4):
        edge = top * (2.0 ** (17 - 8 * i))
        a = (x + edge) - edge
        out.append(a.astype(BF16))
        x = x - a
    return out


def half_gram(s, top, rows):
    tn = ((0,), (0,))
    h = l = low = None
    for at in range(0, s.shape[0], rows):
        a = grid_slices(s[at : at + rows, :], top)
        terms = [0.5 * dot16(a[0], a[0], tn), dot16(a[0], a[1], tn)]
        rest = (dot16(a[0], a[2], tn) + 0.5 * dot16(a[1], a[1], tn)) + (
            (dot16(a[0], a[3], tn) + dot16(a[1], a[2], tn)) + (dot16(a[1], a[3], tn) + 0.5 * dot16(a[2], a[2], tn))
        )
        low = rest if low is None else low + rest
        for t in terms:
            if h is None:
                h = t
            else:
                h, e = two_sum(h, t)
                low = low + e
    return two_sum(h, low)


def local_kernel(corpus_ref, sketch_ref, sample_ref, mine_ref, other_ref, k0_ref, k1_ref, k2_ref, s_ref, x_ref):
    step = pl.program_id(0)

    @pl.when(step == 0)
    def _():
        k0_ref[...], k1_ref[...], k2_ref[...] = split3(sketch_ref[...])
        x_ref[:, 512:] = jnp.zeros((256, 1024), F32)

    c0, c1, c2 = split3(corpus_ref[...])
    k0, k1, k2 = k0_ref[...], k1_ref[...], k2_ref[...]
    s = dot16(c0, k0) + ((dot16(c0, k1) + dot16(c1, k0)) + (dot16(c0, k2) + dot16(c1, k1) + dot16(c2, k0)))
    sample_ref[...] = s
    at = pl.multiple_of(step * ROWS_PER_STEP, ROWS_PER_STEP)
    s_ref[pl.ds(at, ROWS_PER_STEP), :] = s
    s0, s1, s2 = split3(s)
    tn = ((0,), (0,))
    w = dot16(s0, c0, tn) + (
        (dot16(s0, c1, tn) + dot16(s1, c0, tn)) + (dot16(s0, c2, tn) + dot16(s1, c1, tn) + dot16(s2, c0, tn))
    )
    x_ref[:, 512:] = x_ref[:, 512:] + w

    @pl.when(step == pl.num_programs(0) - 1)
    def _():
        top = jnp.max(jnp.abs(s_ref[...]), axis=0, keepdims=True)
        h, l = half_gram(s_ref, top, 1024)
        hi, e = two_sum(h, h.T)
        hi, lo = two_sum(hi, (l + l.T) + e)
        x_ref[:, :256] = hi
        x_ref[:, 256:512] = lo
        core = lax.axis_index(CORE)
        mine_ref[...] = x_ref[pl.ds(pl.multiple_of(core * 128, 128), 128), :]
        other_ref[...] = x_ref[pl.ds(pl.multiple_of((1 - core) * 128, 128), 128), :]


def local_terms(corpus, sketch):
    rows, width = corpus.shape
    cols = sketch.shape[1]
    half = jax.ShapeDtypeStruct((128, 1536), F32)
    return pl.pallas_call(
        local_kernel,
        grid=(rows // ROWS_PER_STEP,),
        in_specs=[
            pl.BlockSpec((ROWS_PER_STEP, width), lambda i: (i, 0)),
            pl.BlockSpec((width, cols), lambda i: (0, 0)),
        ],
        out_specs=[
            pl.BlockSpec((ROWS_PER_STEP, cols), lambda i: (i, 0)),
            pl.BlockSpec((128, 1536), lambda i: (0, 0)),
            pl.BlockSpec((128, 1536), lambda i: (0, 0)),
        ],
        out_shape=[jax.ShapeDtypeStruct((rows, cols), F32), half, half],
        scratch_shapes=[pltpu.VMEM((width, cols), BF16)] * 3
        + [pltpu.VMEM((rows, cols), F32), pltpu.VMEM((256, 1536), F32)],
        name="local_terms",
    )(corpus, sketch)


def added(parts):
    hi, lo, w = parts[0][:, :256], parts[0][:, 256:512], parts[0][:, 512:]
    for p in parts[1:]:
        hi, e = two_sum(hi, p[:, :256])
        lo = lo + (p[:, 256:512] + e)
        w = w + p[:, 512:]
    hi, lo = two_sum(hi, lo)
    return hi, lo, w


def pair_kernel(a_ref, b_ref, out_ref):
    out_ref[:, :256], out_ref[:, 256:512], out_ref[:, 512:] = added([a_ref[...], b_ref[...]])


def pair_sum(a, b):
    return pl.pallas_call(pair_kernel, out_shape=jax.ShapeDtypeStruct(a.shape, F32), name="pair_sum")(a, b)


def stack_kernel(x_ref, out_ref):
    hi, lo, w = added([x_ref[i] for i in range(x_ref.shape[0])])
    for i in range(out_ref.shape[0]):
        out_ref[i, :, :256], out_ref[i, :, 256:512], out_ref[i, :, 512:] = hi, lo, w


def stack_sum(x, copies):
    return pl.pallas_call(
        stack_kernel, out_shape=jax.ShapeDtypeStruct((copies, *x.shape[1:]), F32), name="stack_sum"
    )(x)


def block_inverse(d):
    b = d.shape[0]
    shape = (8, 2 * b)
    row, col = (lax.broadcasted_iota(jnp.int32, (b, b), i) for i in (0, 1))
    m = jnp.concatenate([d, (row == col).astype(F32)], axis=1)
    nt = b // 8
    tiles = [m[8 * t : 8 * t + 8] for t in range(nt)]
    sub = lax.broadcasted_iota(jnp.int32, shape, 0)
    for t in range(nt):
        u = [jnp.broadcast_to(tiles[t][i : i + 1, :], shape) for i in range(8)]
        s = {
            (i, j): jnp.broadcast_to(u[i][:, 8 * t + j : 8 * t + j + 1], shape) for i in range(8) for j in range(i, 8)
        }
        l, rho = {}, []
        for k in range(8):
            rho.append(lax.rsqrt(s[k, k]))
            for i in range(k + 1, 8):
                l[i, k] = s[k, i] * rho[k]
            for i in range(k + 1, 8):
                for j in range(i, 8):
                    s[i, j] = s[i, j] - l[i, k] * l[j, k]
            u[k] = u[k] * rho[k]
            for i in range(k + 1, 8):
                u[i] = u[i] - l[i, k] * u[k]
        out = u[0]
        for k in range(1, 8):
            out = jnp.where(sub == k, u[k], out)
        if t + 1 < nt:
            z = list(u)
            for k in range(7, -1, -1):
                z[k] = z[k] * rho[k]
                for i in range(k):
                    z[i] = z[i] - l[k, i] * z[k]
            for v in range(t + 1, nt):
                p = [jnp.broadcast_to(tiles[v][:, 8 * t + k : 8 * t + k + 1], shape) * z[k] for k in range(8)]
                while len(p) > 1:
                    p = [p[i] + p[i + 1] for i in range(0, len(p), 2)]
                tiles[v] = tiles[v] - p[0]
        tiles[t] = out
    return jnp.concatenate(tiles, axis=0)[:, b:]


def factor_kernel(root, near_ref, far_ref, inverse_ref, projection_ref, g_ref, w_ref, r_ref, y_ref, a_ref, m_ref, u_ref):
    n = 256
    core = lax.axis_index(CORE)
    for ref, half in ((near_ref, core), (far_ref, 1 - core)):
        at = pl.multiple_of(half * 128, 128)
        g_ref[pl.ds(at, 128), :] = ref[:, :512]
        w_ref[pl.ds(at, 128), :] = ref[:, 512:]
    row, col = (lax.broadcasted_iota(jnp.int32, (n, n), i) for i in (0, 1))
    eye = (row == col).astype(F32)
    lower = jnp.where(row > col, 1.0, jnp.where(row == col, 0.5, 0.0))

    a_ref[:, :n] = g_ref[:, :n]
    a_ref[:, n:] = eye
    r_ref[...] = jnp.zeros((n, n), F32)
    for lo in range(0, n, BLOCK):
        hi = lo + BLOCK
        p = dot(block_inverse(a_ref[lo:hi, lo:hi]), a_ref[lo:hi, :])
        r_ref[lo:hi, :] = p[:, :n]
        y_ref[lo:hi, :] = p[:, n:]
        if hi < n:
            a_ref[hi:, :] = a_ref[hi:, :] - dot(p[:, hi:n], p, ((0,), (0,)))
    r = jnp.where(row <= col, r_ref[...], 0.0)
    y = y_ref[...]

    tn, nt = ((0,), (0,)), ((1,), (1,))
    a = grid_slices(r, jnp.max(jnp.abs(r), axis=0, keepdims=True))
    both = lambda i, j: dot16(a[i], a[j], tn) + dot16(a[j], a[i], tn)
    d, e1 = two_sum(g_ref[:, :n], -dot16(a[0], a[0], tn))
    d, e2 = two_sum(d, -both(0, 1))
    fine = both(0, 2) + dot16(a[1], a[1], tn) + ((both(0, 3) + both(1, 2)) + (both(1, 3) + dot16(a[2], a[2], tn)))
    d = d + ((g_ref[:, n:] - fine) + (e1 + e2))

    f = dot(r, y, nt) - eye
    m = eye + ((f + f.T) + dot(f, f, tn) + dot(dot(y, d), y, nt))
    m_ref[...] = m
    u_ref[...] = eye - lower * (m - eye)

    def refine(carry):
        count, _ = carry
        u = u_ref[...]
        off = dot(dot(u, m_ref[...]), u, nt) - eye
        u_ref[...] = u - dot(lower * off, u)
        return count + 1, jnp.max(jnp.abs(off))

    lax.while_loop(lambda c: (c[0] < 24) & (c[1] > 1e-4), refine, (0, jnp.float32(1.0)))
    y = dot(u_ref[...], y)
    inverse_ref[...] = y * root
    projection_ref[...] = dot(y * (1.0 / root), w_ref[...])


def factored(near, far, root):
    import functools

    n = 256
    return pl.pallas_call(
        functools.partial(factor_kernel, root),
        out_shape=[jax.ShapeDtypeStruct((n, n), F32), jax.ShapeDtypeStruct((n, 1024), F32)],
        scratch_shapes=[
            pltpu.VMEM(s, F32) for s in ((n, 512), (n, 1024), (n, n), (n, n), (n, 512), (n, n), (n, n))
        ],
        name="factored",
    )(near, far)


def exchanged(x, axis):
    return lax.all_to_all(x, axis, 0, 0, tiled=True)


def on_device(corpus, sketch):
    plane, line = lax.axis_size(PLANE), lax.axis_size(LINE)
    total_rows = corpus.shape[0] * plane * line * lax.axis_size(CORE)
    root = math.sqrt(total_rows)
    swap = [(0, 1), (1, 0)]
    sample, mine, other = local_terms(corpus, sketch)
    own = pair_sum(mine, lax.ppermute(other, CORE, swap))
    piece = stack_sum(exchanged(own.reshape(plane, 8, 1536), PLANE), line)
    whole = stack_sum(exchanged(piece, LINE), plane)
    near = exchanged(whole, PLANE).reshape(128, 1536)
    far = lax.ppermute(near, CORE, swap)
    inverse, projection = factored(near, far, root)
    basis = dot(sample, inverse, ((1,), (1,)))
    return (basis, projection)


def solution(mesh):
    finer = Mesh(
        mesh.devices.reshape(4, 4, 2, mesh.shape["narrow"]),
        ("wide_0", "wide_1", "wide_2", "narrow"),
    )
    in_specs = (P(WIDE_NARROW, None), P())
    out_specs = (P(WIDE_NARROW, None), P())
    return jax.shard_map(on_device, mesh=finer, in_specs=in_specs, out_specs=out_specs, check_vma=False)
```

profile of v0, /device:TPU:1, one launch (start us, length us, event | category | flops | bytes accessed | tf_op | source)
XLA Modules:
  0.0 130.8 jit_solution(13801112574213882366)
XLA Ops:
  0.6 34.0 %local_terms.1 = (f32[2048,256]{1,0:T(8,128)}, f32[128,1536]{1,0:T(8,128)}, f32[128,1536]{1,0:T(8,128)}) custom-call(f32[2048,1024]{1,0:T(8,128)} %corpus_ref.1, f32[1024,256]{1,0:T(8,128)} %sketch_ref.1), custom_call_target="tpu_custom_call" | custom-call | tf_op jit(solution)/shard_map/local_terms/pallas_call | solution.py:110
  34.6 3.2 %collective-permute-start = (f32[128,1536]{1,0:T(8,128)}, f32[128,1536]{1,0:T(8,128)S(1)}, u32[]{:S(2)}, u32[]{:S(2)}) collective-permute-start(f32[128,1536]{1,0:T(8,128)} %get-tuple-element.9), channel_id=1, source_target_pairs={{0,8},{8,0},{1,9},{9,1},{2,10},{10,2},{3,11},{11,3},{4,12},{12,4},... | collective-permute-start | bytes 2359304 | tf_op jit(solution)/shard_map/ppermute | solution.py:275
  37.8 2.1 %collective-permute-done.b_ref = f32[128,1536]{1,0:T(8,128)S(1)} collective-permute-done((f32[128,1536]{1,0:T(8,128)}, f32[128,1536]{1,0:T(8,128)S(1)}, u32[]{:S(2)}, u32[]{:S(2)}) %collective-permute-start) | collective-permute-done | bytes 786464 | tf_op jit(solution)/shard_map/ppermute | solution.py:275
  39.9 0.0 copy-start.2
  39.9 0.9 copy-done.2
  40.8 2.4 %pair_sum.1 = f32[128,1536]{1,0:T(8,128)} custom-call(f32[128,1536]{1,0:T(8,128)} %get-tuple-element.8.a_ref, f32[128,1536]{1,0:T(8,128)} %copy-done.2), custom_call_target="tpu_custom_call" | custom-call | tf_op jit(solution)/shard_map/pair_sum/pallas_call | solution.py:144
  43.2 18.5 %all_to_all.15.x_ref = f32[16,8,1536]{2,1,0:T(8,128)} all-to-all(f32[16,8,1536]{2,1,0:T(8,128)} %bitcast.6), channel_id=1, replica_groups=mesh['wide_0'=4,'wide_1'=4,'wide_2'=2,'narrow'=8] {'wide_0','wide_1'}, dimensions={0} | all-to-all | bytes 1572864 | tf_op jit(solution)/shard_map/all_to_all | solution.py:266
  61.6 1.9 %stack_sum.2 = f32[8,8,1536]{2,1,0:T(8,128)} custom-call(f32[16,8,1536]{2,1,0:T(8,128)} %all_to_all.15.x_ref), custom_call_target="tpu_custom_call" | custom-call | tf_op jit(solution)/shard_map/stack_sum/pallas_call | solution.py:154
  63.6 20.0 %all_to_all.16.x_ref = f32[8,8,1536]{2,1,0:T(8,128)} all-to-all(f32[8,8,1536]{2,1,0:T(8,128)} %stack_sum.2), channel_id=1, replica_groups=mesh['wide_0'=4,'wide_1'=4,'wide_2'=2,'narrow'=8] {'narrow'}, dimensions={0} | all-to-all | bytes 786432 | tf_op jit(solution)/shard_map/all_to_all | solution.py:266
  83.6 0.0 copy-start.1
  83.6 2.1 %stack_sum.3 = f32[16,8,1536]{2,1,0:T(8,128)} custom-call(f32[8,8,1536]{2,1,0:T(8,128)} %all_to_all.16.x_ref), custom_call_target="tpu_custom_call" | custom-call | tf_op jit(solution)/shard_map/stack_sum/pallas_call | solution.py:154
  85.7 14.8 %all_to_all.17 = f32[16,8,1536]{2,1,0:T(8,128)S(1)} all-to-all(f32[16,8,1536]{2,1,0:T(8,128)} %stack_sum.3), channel_id=1, replica_groups=mesh['wide_0'=4,'wide_1'=4,'wide_2'=2,'narrow'=8] {'wide_0','wide_1'}, dimensions={0} | all-to-all | bytes 1572864 | tf_op jit(solution)/shard_map/all_to_all | solution.py:266
  100.5 0.0 copy-start
  100.5 4.7 %collective-permute-start.1 = (f32[128,1536]{1,0:T(8,128)S(1)}, f32[128,1536]{1,0:T(8,128)}, u32[]{:S(2)}, u32[]{:S(2)}) collective-permute-start(f32[128,1536]{1,0:T(8,128)S(1)} %bitcast.4), channel_id=1, source_target_pairs={{0,8},{8,0},{1,9},{9,1},{2,10},{10,2},{3,11},{11,3},{4,12},{12,4},... | collective-permute-start | bytes 2359304 | tf_op jit(solution)/shard_map/ppermute | solution.py:279
  105.2 2.0 %collective-permute-done.1.far_ref = f32[128,1536]{1,0:T(8,128)} collective-permute-done((f32[128,1536]{1,0:T(8,128)S(1)}, f32[128,1536]{1,0:T(8,128)}, u32[]{:S(2)}, u32[]{:S(2)}) %collective-permute-start.1) | collective-permute-done | bytes 786464 | tf_op jit(solution)/shard_map/ppermute | solution.py:279
  107.3 0.0 copy-done
  107.3 19.5 %factored.1 = (f32[256,256]{1,0:T(8,128)}, f32[256,1024]{1,0:T(8,128)}) custom-call(f32[128,1536]{1,0:T(8,128)} %bitcast.5, f32[128,1536]{1,0:T(8,128)} %collective-permute-done.1.far_ref), custom_call_target="tpu_custom_call" | custom-call | tf_op jit(solution)/shard_map/factored/pallas_call | solution.py:255
  126.7 0.0 copy-done.1
  126.7 4.1 %fusion = f32[2048,256]{1,0:T(8,128)} fusion(f32[2048,256]{1,0:T(8,128)S(1)} %copy-done.1, f32[256,256]{1,0:T(8,128)} %get-tuple-element.10), kind=kOutput, calls=%fused_computation | convolution fusion | flops 1610612736 | bytes 4456448 | tf_op jit(solution)/shard_map/dot_general | solution.py:23
Async XLA Ops:
  34.6 5.3 %collective-permute-start = (f32[128,1536]{1,0:T(8,128)}, f32[128,1536]{1,0:T(8,128)S(1)}, u32[]{:S(2)}, u32[]{:S(2)}) collective-permute-start(f32[128,1536]{1,0:T(8,128)} %get-tuple-element.9), channel_id=1, source_target_pairs={{0,8},{8,0},{1,9},{9,1},{2,10},{10,2},{3,11},{11,3},{4,12},{12,4},... | collective-permute-start | bytes 2359304 | tf_op jit(solution)/shard_map/ppermute | solution.py:275
  39.9 0.9 copy-start.2
  83.6 43.2 %copy-start.1 = (f32[2048,256]{1,0:T(8,128)S(1)}, f32[2048,256]{1,0:T(8,128)}, u32[]{:S(2)}) copy-start(f32[2048,256]{1,0:T(8,128)} %get-tuple-element.7) | copy-start | bytes 6291460
  100.5 6.8 %copy-start = (f32[16,8,1536]{2,1,0:T(8,128)}, f32[16,8,1536]{2,1,0:T(8,128)S(1)}, u32[]{:S(2)}) copy-start(f32[16,8,1536]{2,1,0:T(8,128)S(1)} %all_to_all.17) | copy-start | bytes 2359300
  100.5 6.8 %collective-permute-start.1 = (f32[128,1536]{1,0:T(8,128)S(1)}, f32[128,1536]{1,0:T(8,128)}, u32[]{:S(2)}, u32[]{:S(2)}) collective-permute-start(f32[128,1536]{1,0:T(8,128)S(1)} %bitcast.4), channel_id=1, source_target_pairs={{0,8},{8,0},{1,9},{9,1},{2,10},{10,2},{3,11},{11,3},{4,12},{12,4},... | collective-permute-start | bytes 2359304 | tf_op jit(solution)/shard_map/ppermute | solution.py:279
where the time goes:
time: 131 us
  Pallas kernels  59.9 us (46%)
  blocking collectives  53.2 us (41%)
  starting transfers between devices  7.94 us (6%)
  waiting for transfers between devices  4.17 us (3%)
  matrix products  4.11 us (3%)
    all_to_all x3, blocking collectives, exchanged(): return lax.all_to_all(x, axis, 0, 0, tiled=True)  53.2 us
    pallas_call x1, Pallas kernels, local_terms(): pl.pallas_call(local_kernel, grid=(rows // ROWS_PER_STEP,), in_specs=[pl....  34 us
    pallas_call x1, Pallas kernels, factored(): pl.pallas_call(functools.partial(factor_kernel, root), out_shape=[jax.Sha...  19.5 us
    ppermute x1, starting transfers between devices, on_device(): far = lax.ppermute(near, CORE, swap)  4.74 us
    dot_general x1, matrix products, dot(): lax.dot_general(a, b, (dims, ((), ())), precision=precision, preferred_el...  4.11 us
    pallas_call x2, Pallas kernels, stack_sum(): pl.pallas_call(stack_kernel, out_shape=jax.ShapeDtypeStruct((copies, *x.s...  4.07 us
    ppermute x1, starting transfers between devices, on_device(): own = pair_sum(mine, lax.ppermute(other, CORE, swap))  3.2 us
  transfers between devices with their start and end apart: 2, of which 2 were waited for; matrix products, arithmetic and copies ran while one was open for 0% of the time, Pallas kernels for 0%

commit v1 on v0

--- a/solution.py
+++ b/solution.py
@@ -1,3 +1,4 @@
+import functools
 import math
 
 import jax
@@ -15,7 +16,6 @@
 HI = lax.Precision.HIGHEST
 F32 = jnp.float32
 BF16 = jnp.bfloat16
-ROWS_PER_STEP = 512
 BLOCK = 64
 
 
@@ -25,13 +25,6 @@
 
 def dot16(a, b, dims=((1,), (0,))):
     return lax.dot_general(a, b, (dims, ((), ())), preferred_element_type=F32)
-
-
-def split3(x):
-    a = x.astype(BF16)
-    r = x - a.astype(F32)
-    b = r.astype(BF16)
-    return a, b, (r - b.astype(F32)).astype(BF16)
 
 
 def two_sum(a, b):
@@ -69,61 +62,34 @@
     return two_sum(h, low)
 
 
-def local_kernel(corpus_ref, sketch_ref, sample_ref, mine_ref, other_ref, k0_ref, k1_ref, k2_ref, s_ref, x_ref):
-    step = pl.program_id(0)
-
-    @pl.when(step == 0)
-    def _():
-        k0_ref[...], k1_ref[...], k2_ref[...] = split3(sketch_ref[...])
-        x_ref[:, 512:] = jnp.zeros((256, 1024), F32)
-
-    c0, c1, c2 = split3(corpus_ref[...])
-    k0, k1, k2 = k0_ref[...], k1_ref[...], k2_ref[...]
-    s = dot16(c0, k0) + ((dot16(c0, k1) + dot16(c1, k0)) + (dot16(c0, k2) + dot16(c1, k1) + dot16(c2, k0)))
-    sample_ref[...] = s
-    at = pl.multiple_of(step * ROWS_PER_STEP, ROWS_PER_STEP)
-    s_ref[pl.ds(at, ROWS_PER_STEP), :] = s
-    s0, s1, s2 = split3(s)
-    tn = ((0,), (0,))
-    w = dot16(s0, c0, tn) + (
-        (dot16(s0, c1, tn) + dot16(s1, c0, tn)) + (dot16(s0, c2, tn) + dot16(s1, c1, tn) + dot16(s2, c0, tn))
-    )
-    x_ref[:, 512:] = x_ref[:, 512:] + w
-
-    @pl.when(step == pl.num_programs(0) - 1)
-    def _():
-        top = jnp.max(jnp.abs(s_ref[...]), axis=0, keepdims=True)
-        h, l = half_gram(s_ref, top, 1024)
-        hi, e = two_sum(h, h.T)
-        hi, lo = two_sum(hi, (l + l.T) + e)
-        x_ref[:, :256] = hi
-        x_ref[:, 256:512] = lo
-        core = lax.axis_index(CORE)
-        mine_ref[...] = x_ref[pl.ds(pl.multiple_of(core * 128, 128), 128), :]
-        other_ref[...] = x_ref[pl.ds(pl.multiple_of((1 - core) * 128, 128), 128), :]
-
-
-def local_terms(corpus, sketch):
-    rows, width = corpus.shape
-    cols = sketch.shape[1]
-    half = jax.ShapeDtypeStruct((128, 1536), F32)
-    return pl.pallas_call(
-        local_kernel,
-        grid=(rows // ROWS_PER_STEP,),
-        in_specs=[
-            pl.BlockSpec((ROWS_PER_STEP, width), lambda i: (i, 0)),
-            pl.BlockSpec((width, cols), lambda i: (0, 0)),
-        ],
-        out_specs=[
-            pl.BlockSpec((ROWS_PER_STEP, cols), lambda i: (i, 0)),
-            pl.BlockSpec((128, 1536), lambda i: (0, 0)),
-            pl.BlockSpec((128, 1536), lambda i: (0, 0)),
-        ],
-        out_shape=[jax.ShapeDtypeStruct((rows, cols), F32), half, half],
-        scratch_shapes=[pltpu.VMEM((width, cols), BF16)] * 3
-        + [pltpu.VMEM((rows, cols), F32), pltpu.VMEM((256, 1536), F32)],
-        name="local_terms",
-    )(corpus, sketch)
+def in_vmem(n):
+    return [pl.BlockSpec(memory_space=pltpu.VMEM)] * n
+
+
+def gram_kernel(sample_ref, terms_ref, mine_ref, other_ref, x_ref):
+    top = jnp.max(jnp.abs(sample_ref[...]), axis=0, keepdims=True)
+    h, l = half_gram(sample_ref, top, 1024)
+    hi, e = two_sum(h, h.T)
+    hi, lo = two_sum(hi, (l + l.T) + e)
+    x_ref[:, :256] = hi
+    x_ref[:, 256:] = lo
+    core = lax.axis_index(CORE)
+    for half, ref in ((core, mine_ref), (1 - core, other_ref)):
+        at = pl.multiple_of(half * 128, 128)
+        ref[:, :512] = x_ref[pl.ds(at, 128), :]
+        ref[:, 512:] = terms_ref[pl.ds(at, 128), :]
+
+
+def local_halves(sample, terms):
+    return pl.pallas_call(
+        gram_kernel,
+        in_specs=in_vmem(2),
+        out_specs=in_vmem(2),
+        out_shape=[jax.ShapeDtypeStruct((128, 1536), F32)] * 2,
+        scratch_shapes=[pltpu.VMEM((256, 512), F32)],
+        compiler_params=pltpu.CompilerParams(vmem_limit_bytes=20 * 2**20),
+        name="local_halves",
+    )(sample, terms)
 
 
 def added(parts):
@@ -141,7 +107,14 @@
 
 
 def pair_sum(a, b):
-    return pl.pallas_call(pair_kernel, out_shape=jax.ShapeDtypeStruct(a.shape, F32), name="pair_sum")(a, b)
+    return pl.pallas_call(
+        pair_kernel,
+        in_specs=in_vmem(2),
+        out_specs=in_vmem(1)[0],
+        out_shape=jax.ShapeDtypeStruct(a.shape, F32),
+        compiler_params=pltpu.CompilerParams(vmem_limit_bytes=6 * 2**20),
+        name="pair_sum",
+    )(a, b)
 
 
 def stack_kernel(x_ref, out_ref):
@@ -152,7 +125,12 @@
 
 def stack_sum(x, copies):
     return pl.pallas_call(
-        stack_kernel, out_shape=jax.ShapeDtypeStruct((copies, *x.shape[1:]), F32), name="stack_sum"
+        stack_kernel,
+        in_specs=in_vmem(1),
+        out_specs=in_vmem(1)[0],
+        out_shape=jax.ShapeDtypeStruct((copies, *x.shape[1:]), F32),
+        compiler_params=pltpu.CompilerParams(vmem_limit_bytes=6 * 2**20),
+        name="stack_sum",
     )(x)
 
 
@@ -244,20 +222,21 @@
 
     lax.while_loop(lambda c: (c[0] < 24) & (c[1] > 1e-4), refine, (0, jnp.float32(1.0)))
     y = dot(u_ref[...], y)
-    inverse_ref[...] = y * root
+    inverse_ref[...] = (y * root).T
     projection_ref[...] = dot(y * (1.0 / root), w_ref[...])
 
 
 def factored(near, far, root):
-    import functools
-
     n = 256
     return pl.pallas_call(
         functools.partial(factor_kernel, root),
+        in_specs=in_vmem(2),
+        out_specs=in_vmem(2),
         out_shape=[jax.ShapeDtypeStruct((n, n), F32), jax.ShapeDtypeStruct((n, 1024), F32)],
         scratch_shapes=[
             pltpu.VMEM(s, F32) for s in ((n, 512), (n, 1024), (n, n), (n, n), (n, 512), (n, n), (n, n))
         ],
+        compiler_params=pltpu.CompilerParams(vmem_limit_bytes=16 * 2**20),
         name="factored",
     )(near, far)
 
@@ -271,14 +250,16 @@
     total_rows = corpus.shape[0] * plane * line * lax.axis_size(CORE)
     root = math.sqrt(total_rows)
     swap = [(0, 1), (1, 0)]
-    sample, mine, other = local_terms(corpus, sketch)
+    sample = dot(corpus, sketch)
+    terms = dot(sample, corpus, ((0,), (0,)), lax.Precision.HIGH)
+    mine, other = local_halves(sample, terms)
     own = pair_sum(mine, lax.ppermute(other, CORE, swap))
     piece = stack_sum(exchanged(own.reshape(plane, 8, 1536), PLANE), line)
     whole = stack_sum(exchanged(piece, LINE), plane)
     near = exchanged(whole, PLANE).reshape(128, 1536)
     far = lax.ppermute(near, CORE, swap)
     inverse, projection = factored(near, far, root)
-    basis = dot(sample, inverse, ((1,), (1,)))
+    basis = dot(sample, inverse)
     return (basis, projection)
 
 

time: 131 us -> 106 us (0.81)
  Pallas kernels: 59.9 us -> 22 us
  matrix products: 4.11 us -> 17.2 us
    pallas_call x5, Pallas kernels: 59.9 us -> 22 us  [the longest x1 18.1 us: factored(): pl.pallas_call(functools.partial(factor_kernel, root), in_specs=in_vmem(2...]
    dot_general x1 -> x3, matrix products: 4.11 us -> 17.2 us  [dot(): lax.dot_general(a, b, (dims, ((), ())), precision=precision, preferred_el...]
where the time goes in v1:
time: 106 us
  blocking collectives  52.6 us (50%)
  Pallas kernels  22 us (21%)
  matrix products  17.2 us (16%)
  starting transfers between devices  8.02 us (8%)
  waiting for transfers between devices  3.82 us (4%)
  local copies, waits for them, and re-layouts  1.23 us (1%)
    all_to_all x3, blocking collectives, exchanged(): return lax.all_to_all(x, axis, 0, 0, tiled=True)  52.6 us
    pallas_call x1, Pallas kernels, factored(): pl.pallas_call(functools.partial(factor_kernel, root), in_specs=in_vmem(2...  18.1 us
    dot_general x3, matrix products, dot(): lax.dot_general(a, b, (dims, ((), ())), precision=precision, preferred_el...  17.2 us
    ppermute x1, starting transfers between devices, on_device(): far = lax.ppermute(near, CORE, swap)  4.74 us
    pallas_call x1, Pallas kernels, local_halves(): pl.pallas_call(gram_kernel, in_specs=in_vmem(2), out_specs=in_vmem(2), ou...  3.59 us
    ppermute x1, starting transfers between devices, on_device(): own = pair_sum(mine, lax.ppermute(other, CORE, swap))  3.29 us
  transfers between devices with their start and end apart: 2, of which 2 were waited for; matrix products, arithmetic and copies ran while one was open for 0% of the time, Pallas kernels for 0%

profile of v1, /device:TPU:1, one launch (start us, length us, event | category | flops | bytes accessed | tf_op | source)
XLA Modules:
  0.0 105.5 jit_solution(12263807048901650718)
XLA Ops:
  0.6 0.0 copy-start
  0.6 1.2 %copy-done = f32[1024,256]{1,0:T(8,128)S(1)} copy-done((f32[1024,256]{1,0:T(8,128)S(1)}, f32[1024,256]{1,0:T(8,128)}, u32[]{:S(2)}) %copy-start) | copy-done | bytes 1048600
  1.9 0.0 copy-start.1
  1.9 9.9 %fusion.sample_ref = f32[2048,256]{1,0:T(8,128)S(1)} fusion(f32[2048,1024]{1,0:T(8,128)} %param.2, f32[1024,256]{1,0:T(8,128)S(1)} %copy-done), kind=kOutput, calls=%fused_computation | convolution fusion | flops 6442450944 | bytes 11534336 | tf_op jit(solution)/shard_map/dot_general | solution.py:23
  11.8 0.0 copy-done.1
  11.8 4.2 %fusion.1.terms_ref = f32[256,1024]{1,0:T(8,128)S(1)} fusion(f32[2048,256]{1,0:T(8,128)S(1)} %fusion.sample_ref, f32[2048,1024]{1,0:T(8,128)S(1)} %copy-done.1), kind=kOutput, calls=%fused_computation.1 | convolution fusion | flops 3221225472 | bytes 11534336 | tf_op jit(solution)/shard_map/dot_general | solution.py:23
  16.0 3.6 %local_halves.1 = (f32[128,1536]{1,0:T(8,128)S(1)}, f32[128,1536]{1,0:T(8,128)S(1)}) custom-call(f32[2048,256]{1,0:T(8,128)S(1)} %fusion.sample_ref, f32[256,1024]{1,0:T(8,128)S(1)} %fusion.1.terms_ref), custom_call_target="tpu_custom_call" | custom-call | tf_op jit(solution)/shard_map/local_halves/pallas_call | solution.py:84
  19.6 3.3 %collective-permute-start = (f32[128,1536]{1,0:T(8,128)S(1)}, f32[128,1536]{1,0:T(8,128)S(1)}, u32[]{:S(2)}, u32[]{:S(2)}) collective-permute-start(f32[128,1536]{1,0:T(8,128)S(1)} %get-tuple-element.7), channel_id=1, source_target_pairs={{0,8},{8,0},{1,9},{9,1},{2,10},{10,2},{3,11},{11,3},{4,12},{12,4},... | collective-permute-start | bytes 2359304 | tf_op jit(solution)/shard_map/ppermute | solution.py:256
  22.9 1.9 %collective-permute-done.b_ref = f32[128,1536]{1,0:T(8,128)S(1)} collective-permute-done((f32[128,1536]{1,0:T(8,128)S(1)}, f32[128,1536]{1,0:T(8,128)S(1)}, u32[]{:S(2)}, u32[]{:S(2)}) %collective-permute-start) | collective-permute-done | bytes 786464 | tf_op jit(solution)/shard_map/ppermute | solution.py:256
  24.8 0.1 pair_sum.1
  24.9 18.2 %all_to_all.15.x_ref = f32[16,8,1536]{2,1,0:T(8,128)S(1)} all-to-all(f32[16,8,1536]{2,1,0:T(8,128)S(1)} %bitcast.10), channel_id=1, replica_groups=mesh['wide_0'=4,'wide_1'=4,'wide_2'=2,'narrow'=8] {'wide_0','wide_1'}, dimensions={0} | all-to-all | bytes 1572864 | tf_op jit(solution)/shard_map/all_to_all | solution.py:245
  43.0 0.1 stack_sum.2
  43.1 19.9 %all_to_all.16.x_ref = f32[8,8,1536]{2,1,0:T(8,128)S(1)} all-to-all(f32[8,8,1536]{2,1,0:T(8,128)S(1)} %stack_sum.2), channel_id=1, replica_groups=mesh['wide_0'=4,'wide_1'=4,'wide_2'=2,'narrow'=8] {'narrow'}, dimensions={0} | all-to-all | bytes 786432 | tf_op jit(solution)/shard_map/all_to_all | solution.py:245
  63.0 0.1 stack_sum.3
  63.1 14.6 %all_to_all.17 = f32[16,8,1536]{2,1,0:T(8,128)S(1)} all-to-all(f32[16,8,1536]{2,1,0:T(8,128)S(1)} %stack_sum.3), channel_id=1, replica_groups=mesh['wide_0'=4,'wide_1'=4,'wide_2'=2,'narrow'=8] {'wide_0','wide_1'}, dimensions={0} | all-to-all | bytes 1572864 | tf_op jit(solution)/shard_map/all_to_all | solution.py:245
  77.6 4.7 %collective-permute-start.1 = (f32[128,1536]{1,0:T(8,128)S(1)}, f32[128,1536]{1,0:T(8,128)S(1)}, u32[]{:S(2)}, u32[]{:S(2)}) collective-permute-start(f32[128,1536]{1,0:T(8,128)S(1)} %bitcast.8), channel_id=1, source_target_pairs={{0,8},{8,0},{1,9},{9,1},{2,10},{10,2},{3,11},{11,3},{4,12},{12,4},... | collective-permute-start | bytes 2359304 | tf_op jit(solution)/shard_map/ppermute | solution.py:260
  82.4 1.9 %collective-permute-done.1.far_ref = f32[128,1536]{1,0:T(8,128)S(1)} collective-permute-done((f32[128,1536]{1,0:T(8,128)S(1)}, f32[128,1536]{1,0:T(8,128)S(1)}, u32[]{:S(2)}, u32[]{:S(2)}) %collective-permute-start.1) | collective-permute-done | bytes 786464 | tf_op jit(solution)/shard_map/ppermute | solution.py:260
  84.3 18.1 %factored.1 = (f32[256,256]{1,0:T(8,128)S(1)}, f32[256,1024]{1,0:T(8,128)}) custom-call(f32[128,1536]{1,0:T(8,128)S(1)} %bitcast.9, f32[128,1536]{1,0:T(8,128)S(1)} %collective-permute-done.1.far_ref), custom_call_target="tpu_custom_call" | custom-call | tf_op jit(solution)/shard_map/factored/pallas_call | solution.py:231
  102.4 3.1 %fusion.2 = f32[2048,256]{1,0:T(8,128)} fusion(f32[2048,256]{1,0:T(8,128)S(1)} %fusion.sample_ref, f32[256,256]{1,0:T(8,128)S(1)} %get-tuple-element.8), kind=kOutput, calls=%fused_computation.2 | convolution fusion | flops 1610612736 | bytes 4456448 | tf_op jit(solution)/shard_map/dot_general | solution.py:23
Async XLA Ops:
  0.6 1.2 %copy-start = (f32[1024,256]{1,0:T(8,128)S(1)}, f32[1024,256]{1,0:T(8,128)}, u32[]{:S(2)}) copy-start(f32[1024,256]{1,0:T(8,128)} %param.3) | copy-start | bytes 3145732
  1.9 10.0 %copy-start.1 = (f32[2048,1024]{1,0:T(8,128)S(1)}, f32[2048,1024]{1,0:T(8,128)}, u32[]{:S(2)}) copy-start(f32[2048,1024]{1,0:T(8,128)} %param.2) | copy-start | bytes 25165828
  19.6 5.2 %collective-permute-start = (f32[128,1536]{1,0:T(8,128)S(1)}, f32[128,1536]{1,0:T(8,128)S(1)}, u32[]{:S(2)}, u32[]{:S(2)}) collective-permute-start(f32[128,1536]{1,0:T(8,128)S(1)} %get-tuple-element.7), channel_id=1, source_target_pairs={{0,8},{8,0},{1,9},{9,1},{2,10},{10,2},{3,11},{11,3},{4,12},{12,4},... | collective-permute-start | bytes 2359304 | tf_op jit(solution)/shard_map/ppermute | solution.py:256
  77.6 6.7 %collective-permute-start.1 = (f32[128,1536]{1,0:T(8,128)S(1)}, f32[128,1536]{1,0:T(8,128)S(1)}, u32[]{:S(2)}, u32[]{:S(2)}) collective-permute-start(f32[128,1536]{1,0:T(8,128)S(1)} %bitcast.8), channel_id=1, source_target_pairs={{0,8},{8,0},{1,9},{9,1},{2,10},{10,2},{3,11},{11,3},{4,12},{12,4},... | collective-permute-start | bytes 2359304 | tf_op jit(solution)/shard_map/ppermute | solution.py:260

commit v2 on v1

--- a/solution.py
+++ b/solution.py
@@ -92,46 +92,37 @@
     )(sample, terms)
 
 
-def added(parts):
-    hi, lo, w = parts[0][:, :256], parts[0][:, 256:512], parts[0][:, 512:]
-    for p in parts[1:]:
-        hi, e = two_sum(hi, p[:, :256])
-        lo = lo + (p[:, 256:512] + e)
-        w = w + p[:, 512:]
-    hi, lo = two_sum(hi, lo)
-    return hi, lo, w
+def plus(a, b):
+    hi, e = two_sum(a[:, :256], b[:, :256])
+    hi, lo = two_sum(hi, (a[:, 256:512] + b[:, 256:512]) + e)
+    return jnp.concatenate([hi, lo, a[:, 512:] + b[:, 512:]], axis=1)
 
 
 def pair_kernel(a_ref, b_ref, out_ref):
-    out_ref[:, :256], out_ref[:, 256:512], out_ref[:, 512:] = added([a_ref[...], b_ref[...]])
-
-
-def pair_sum(a, b):
+    s = plus(a_ref[...], b_ref[...])
+    if len(out_ref.shape) == 2:
+        out_ref[...] = s
+    else:
+        for i in range(out_ref.shape[0]):
+            out_ref[i] = s
+
+
+def stack_kernel(x_ref, out_ref):
+    parts = [x_ref[i] for i in range(x_ref.shape[0])]
+    while len(parts) > 1:
+        parts = [plus(parts[i], parts[i + 1]) for i in range(0, len(parts), 2)]
+    out_ref[...] = parts[0]
+
+
+def added(kernel, shape, name, *parts):
     return pl.pallas_call(
-        pair_kernel,
-        in_specs=in_vmem(2),
+        kernel,
+        in_specs=in_vmem(len(parts)),
         out_specs=in_vmem(1)[0],
-        out_shape=jax.ShapeDtypeStruct(a.shape, F32),
+        out_shape=jax.ShapeDtypeStruct(shape, F32),
         compiler_params=pltpu.CompilerParams(vmem_limit_bytes=6 * 2**20),
-        name="pair_sum",
-    )(a, b)
-
-
-def stack_kernel(x_ref, out_ref):
-    hi, lo, w = added([x_ref[i] for i in range(x_ref.shape[0])])
-    for i in range(out_ref.shape[0]):
-        out_ref[i, :, :256], out_ref[i, :, 256:512], out_ref[i, :, 512:] = hi, lo, w
-
-
-def stack_sum(x, copies):
-    return pl.pallas_call(
-        stack_kernel,
-        in_specs=in_vmem(1),
-        out_specs=in_vmem(1)[0],
-        out_shape=jax.ShapeDtypeStruct((copies, *x.shape[1:]), F32),
-        compiler_params=pltpu.CompilerParams(vmem_limit_bytes=6 * 2**20),
-        name="stack_sum",
-    )(x)
+        name=name,
+    )(*parts)
 
 
 def block_inverse(d):
@@ -143,35 +134,30 @@
     tiles = [m[8 * t : 8 * t + 8] for t in range(nt)]
     sub = lax.broadcasted_iota(jnp.int32, shape, 0)
     for t in range(nt):
+        across = lambda x, j: jnp.broadcast_to(x[:, 8 * t + j : 8 * t + j + 1], shape)
         u = [jnp.broadcast_to(tiles[t][i : i + 1, :], shape) for i in range(8)]
-        s = {
-            (i, j): jnp.broadcast_to(u[i][:, 8 * t + j : 8 * t + j + 1], shape) for i in range(8) for j in range(i, 8)
-        }
-        l, rho = {}, []
+        s = {(i, j): across(u[i], j) for i in range(8) for j in range(i, 8)}
+        below = {v: [across(tiles[v], k) for k in range(8)] for v in range(t + 1, nt)}
+        l = {}
         for k in range(8):
-            rho.append(lax.rsqrt(s[k, k]))
+            rho = lax.rsqrt(s[k, k])
             for i in range(k + 1, 8):
-                l[i, k] = s[k, i] * rho[k]
+                l[i] = s[k, i] * rho
             for i in range(k + 1, 8):
                 for j in range(i, 8):
-                    s[i, j] = s[i, j] - l[i, k] * l[j, k]
-            u[k] = u[k] * rho[k]
-            for i in range(k + 1, 8):
-                u[i] = u[i] - l[i, k] * u[k]
+                    s[i, j] = s[i, j] - l[i] * l[j]
+            for w in [u, *below.values()]:
+                w[k] = w[k] * rho
+                for i in range(k + 1, 8):
+                    w[i] = w[i] - l[i] * w[k]
         out = u[0]
         for k in range(1, 8):
             out = jnp.where(sub == k, u[k], out)
-        if t + 1 < nt:
-            z = list(u)
-            for k in range(7, -1, -1):
-                z[k] = z[k] * rho[k]
-                for i in range(k):
-                    z[i] = z[i] - l[k, i] * z[k]
-            for v in range(t + 1, nt):
-                p = [jnp.broadcast_to(tiles[v][:, 8 * t + k : 8 * t + k + 1], shape) * z[k] for k in range(8)]
-                while len(p) > 1:
-                    p = [p[i] + p[i + 1] for i in range(0, len(p), 2)]
-                tiles[v] = tiles[v] - p[0]
+        for v, w in below.items():
+            p = [w[k] * u[k] for k in range(8)]
+            while len(p) > 1:
+                p = [p[i] + p[i + 1] for i in range(0, len(p), 2)]
+            tiles[v] = tiles[v] - p[0]
         tiles[t] = out
     return jnp.concatenate(tiles, axis=0)[:, b:]
 
@@ -253,9 +239,14 @@
     sample = dot(corpus, sketch)
     terms = dot(sample, corpus, ((0,), (0,)), lax.Precision.HIGH)
     mine, other = local_halves(sample, terms)
-    own = pair_sum(mine, lax.ppermute(other, CORE, swap))
-    piece = stack_sum(exchanged(own.reshape(plane, 8, 1536), PLANE), line)
-    whole = stack_sum(exchanged(piece, LINE), plane)
+    own = added(pair_kernel, mine.shape, "pair_sum", mine, lax.ppermute(other, CORE, swap))
+    whole = added(stack_kernel, (8, 1536), "stack_sum", exchanged(own.reshape(plane, 8, 1536), PLANE))
+    far = 1
+    while far < line:
+        arrived = lax.ppermute(whole, LINE, [(i, i ^ far) for i in range(line)])
+        far *= 2
+        out = (8, 1536) if far < line else (plane, 8, 1536)
+        whole = added(pair_kernel, out, "pair_sum", whole, arrived)
     near = exchanged(whole, PLANE).reshape(128, 1536)
     far = lax.ppermute(near, CORE, swap)
     inverse, projection = factored(near, far, root)

time: 106 us -> 100 us (0.943)
  blocking collectives: 52.6 us -> 32 us
  starting transfers between devices: 8.02 us -> 20.8 us
  waiting for transfers between devices: 3.82 us -> 8.38 us
  Pallas kernels: 22 us -> 19.8 us
    all_to_all x3 -> x2, blocking collectives: 52.6 us -> 32 us  [exchanged(): return lax.all_to_all(x, axis, 0, 0, tiled=True)]
    ppermute x1 -> x4, starting transfers between devices: 3.29 us -> 14.5 us  [the longest x3 11.2 us: on_device(): arrived = lax.ppermute(whole, LINE, [(i, i ^ far) for i in range(line)])]
    ppermute x1 -> x4, waiting for transfers between devices: 1.91 us -> 6.47 us  [the longest x3 4.56 us: on_device(): arrived = lax.ppermute(whole, LINE, [(i, i ^ far) for i in range(line)])]
    pallas_call x1, Pallas kernels: 18.1 us -> 16 us  [factored(): pl.pallas_call(functools.partial(factor_kernel, root), in_specs=in_vmem(2...]
    ppermute x1, starting transfers between devices: 4.74 us -> 6.3 us  [on_device(): far = lax.ppermute(near, CORE, swap)]
  transfers between devices with their start and end apart: 2 -> 5, of which waited for: 2 -> 5; matrix products, arithmetic and copies ran while one was open for 0% -> 0% of each run, Pallas kernels for 0% -> 0%
where the time goes in v2:
time: 100 us
  blocking collectives  32 us (32%)
  starting transfers between devices  20.8 us (21%)
  Pallas kernels  19.8 us (20%)
  matrix products  17.2 us (17%)
  waiting for transfers between devices  8.38 us (8%)
  local copies, waits for them, and re-layouts  1.23 us (1%)
    all_to_all x2, blocking collectives, exchanged(): return lax.all_to_all(x, axis, 0, 0, tiled=True)  32 us
    dot_general x3, matrix products, dot(): lax.dot_general(a, b, (dims, ((), ())), precision=precision, preferred_el...  17.2 us
    pallas_call x1, Pallas kernels, factored(): pl.pallas_call(functools.partial(factor_kernel, root), in_specs=in_vmem(2...  16 us
    ppermute x3, starting transfers between devices, on_device(): arrived = lax.ppermute(whole, LINE, [(i, i ^ far) for i in range(line)])  11.2 us
    ppermute x1, starting transfers between devices, on_device(): far = lax.ppermute(near, CORE, swap)  6.3 us
    ppermute x3, waiting for transfers between devices, on_device(): arrived = lax.ppermute(whole, LINE, [(i, i ^ far) for i in range(line)])  4.56 us
    pallas_call x1, Pallas kernels, local_halves(): pl.pallas_call(gram_kernel, in_specs=in_vmem(2), out_specs=in_vmem(2), ou...  3.59 us
    ppermute x1, starting transfers between devices, on_device(): lax.ppermute(other, CORE, swap)  3.29 us
  transfers between devices with their start and end apart: 5, of which 5 were waited for; matrix products, arithmetic and copies ran while one was open for 0% of the time, Pallas kernels for 0%

profile of v2, /device:TPU:1, one launch (start us, length us, event | category | flops | bytes accessed | tf_op | source)
XLA Modules:
  0.0 100.1 jit_solution(11679723647741299144)
XLA Ops:
  0.6 0.0 copy-start
  0.6 1.2 %copy-done = f32[1024,256]{1,0:T(8,128)S(1)} copy-done((f32[1024,256]{1,0:T(8,128)S(1)}, f32[1024,256]{1,0:T(8,128)}, u32[]{:S(2)}) %copy-start) | copy-done | bytes 1048600
  1.9 0.0 copy-start.1
  1.9 9.9 %fusion.sample_ref = f32[2048,256]{1,0:T(8,128)S(1)} fusion(f32[2048,1024]{1,0:T(8,128)} %param.2, f32[1024,256]{1,0:T(8,128)S(1)} %copy-done), kind=kOutput, calls=%fused_computation | convolution fusion | flops 6442450944 | bytes 11534336 | tf_op jit(solution)/shard_map/dot_general | solution.py:23
  11.8 0.0 copy-done.1
  11.8 4.2 %fusion.1.terms_ref = f32[256,1024]{1,0:T(8,128)S(1)} fusion(f32[2048,256]{1,0:T(8,128)S(1)} %fusion.sample_ref, f32[2048,1024]{1,0:T(8,128)S(1)} %copy-done.1), kind=kOutput, calls=%fused_computation.1 | convolution fusion | flops 3221225472 | bytes 11534336 | tf_op jit(solution)/shard_map/dot_general | solution.py:23
  16.0 3.6 %local_halves.1 = (f32[128,1536]{1,0:T(8,128)S(1)}, f32[128,1536]{1,0:T(8,128)S(1)}) custom-call(f32[2048,256]{1,0:T(8,128)S(1)} %fusion.sample_ref, f32[256,1024]{1,0:T(8,128)S(1)} %fusion.1.terms_ref), custom_call_target="tpu_custom_call" | custom-call | tf_op jit(solution)/shard_map/local_halves/pallas_call | solution.py:84
  19.6 3.3 %collective-permute-start = (f32[128,1536]{1,0:T(8,128)S(1)}, f32[128,1536]{1,0:T(8,128)S(1)}, u32[]{:S(2)}, u32[]{:S(2)}) collective-permute-start(f32[128,1536]{1,0:T(8,128)S(1)} %get-tuple-element.7), channel_id=1, source_target_pairs={{0,8},{8,0},{1,9},{9,1},{2,10},{10,2},{3,11},{11,3},{4,12},{12,4},... | collective-permute-start | bytes 2359304 | tf_op jit(solution)/shard_map/ppermute | solution.py:242
  22.9 1.9 %collective-permute-done.b_ref = f32[128,1536]{1,0:T(8,128)S(1)} collective-permute-done((f32[128,1536]{1,0:T(8,128)S(1)}, f32[128,1536]{1,0:T(8,128)S(1)}, u32[]{:S(2)}, u32[]{:S(2)}) %collective-permute-start) | collective-permute-done | bytes 786464 | tf_op jit(solution)/shard_map/ppermute | solution.py:242
  24.8 0.1 pair_sum.4
  24.9 18.2 %all_to_all.10.x_ref = f32[16,8,1536]{2,1,0:T(8,128)S(1)} all-to-all(f32[16,8,1536]{2,1,0:T(8,128)S(1)} %bitcast.10), channel_id=1, replica_groups=mesh['wide_0'=4,'wide_1'=4,'wide_2'=2,'narrow'=8] {'wide_0','wide_1'}, dimensions={0} | all-to-all | bytes 1572864 | tf_op jit(solution)/shard_map/all_to_all | solution.py:231
  43.0 0.1 stack_sum.1.a_ref
  43.1 1.9 %collective-permute-start.1 = (f32[8,1536]{1,0:T(8,128)S(1)}, f32[8,1536]{1,0:T(8,128)S(1)}, u32[]{:S(2)}, u32[]{:S(2)}) collective-permute-start(f32[8,1536]{1,0:T(8,128)S(1)} %stack_sum.1.a_ref), channel_id=1, source_target_pairs={{0,1},{1,0},{2,3},{3,2},{4,5},{5,4},{6,7},{7,6},{8,9},{9,8},{10,11... | collective-permute-start | bytes 147464 | tf_op jit(solution)/shard_map/ppermute | solution.py:246
  45.0 1.5 %collective-permute-done.1.b_ref = f32[8,1536]{1,0:T(8,128)S(1)} collective-permute-done((f32[8,1536]{1,0:T(8,128)S(1)}, f32[8,1536]{1,0:T(8,128)S(1)}, u32[]{:S(2)}, u32[]{:S(2)}) %collective-permute-start.1) | collective-permute-done | bytes 49184 | tf_op jit(solution)/shard_map/ppermute | solution.py:246
  46.5 3.1 %collective-permute-start.2 = (f32[8,1536]{1,0:T(8,128)S(1)}, f32[8,1536]{1,0:T(8,128)S(1)}, u32[]{:S(2)}, u32[]{:S(2)}) collective-permute-start(f32[8,1536]{1,0:T(8,128)S(1)} %pair_sum.5.a_ref), channel_id=1, source_target_pairs={{0,2},{1,3},{2,0},{3,1},{4,6},{5,7},{6,4},{7,5},{8,10},{9,11},{10,... | collective-permute-start | bytes 147464 | tf_op jit(solution)/shard_map/ppermute | solution.py:246
  49.6 1.5 %collective-permute-done.2.b_ref = f32[8,1536]{1,0:T(8,128)S(1)} collective-permute-done((f32[8,1536]{1,0:T(8,128)S(1)}, f32[8,1536]{1,0:T(8,128)S(1)}, u32[]{:S(2)}, u32[]{:S(2)}) %collective-permute-start.2) | collective-permute-done | bytes 49184 | tf_op jit(solution)/shard_map/ppermute | solution.py:246
  51.1 6.2 %collective-permute-start.3 = (f32[8,1536]{1,0:T(8,128)S(1)}, f32[8,1536]{1,0:T(8,128)S(1)}, u32[]{:S(2)}, u32[]{:S(2)}) collective-permute-start(f32[8,1536]{1,0:T(8,128)S(1)} %pair_sum.6.a_ref), channel_id=1, source_target_pairs={{0,4},{1,5},{2,6},{3,7},{4,0},{5,1},{6,2},{7,3},{8,12},{9,13},{10,... | collective-permute-start | bytes 147464 | tf_op jit(solution)/shard_map/ppermute | solution.py:246
  57.3 1.6 %collective-permute-done.3.b_ref = f32[8,1536]{1,0:T(8,128)S(1)} collective-permute-done((f32[8,1536]{1,0:T(8,128)S(1)}, f32[8,1536]{1,0:T(8,128)S(1)}, u32[]{:S(2)}, u32[]{:S(2)}) %collective-permute-start.3) | collective-permute-done | bytes 49184 | tf_op jit(solution)/shard_map/ppermute | solution.py:246
  58.9 0.1 pair_sum.7
  59.0 13.8 %all_to_all.11 = f32[16,8,1536]{2,1,0:T(8,128)S(1)} all-to-all(f32[16,8,1536]{2,1,0:T(8,128)S(1)} %pair_sum.7), channel_id=1, replica_groups=mesh['wide_0'=4,'wide_1'=4,'wide_2'=2,'narrow'=8] {'wide_0','wide_1'}, dimensions={0} | all-to-all | bytes 1572864 | tf_op jit(solution)/shard_map/all_to_all | solution.py:231
  72.8 6.3 %collective-permute-start.4 = (f32[128,1536]{1,0:T(8,128)S(1)}, f32[128,1536]{1,0:T(8,128)S(1)}, u32[]{:S(2)}, u32[]{:S(2)}) collective-permute-start(f32[128,1536]{1,0:T(8,128)S(1)} %bitcast.8), channel_id=1, source_target_pairs={{0,8},{8,0},{1,9},{9,1},{2,10},{10,2},{3,11},{11,3},{4,12},{12,4},... | collective-permute-start | bytes 2359304 | tf_op jit(solution)/shard_map/ppermute | solution.py:251
  79.1 1.9 %collective-permute-done.4.far_ref = f32[128,1536]{1,0:T(8,128)S(1)} collective-permute-done((f32[128,1536]{1,0:T(8,128)S(1)}, f32[128,1536]{1,0:T(8,128)S(1)}, u32[]{:S(2)}, u32[]{:S(2)}) %collective-permute-start.4) | collective-permute-done | bytes 786464 | tf_op jit(solution)/shard_map/ppermute | solution.py:251
  81.0 16.0 %factored.1 = (f32[256,256]{1,0:T(8,128)S(1)}, f32[256,1024]{1,0:T(8,128)}) custom-call(f32[128,1536]{1,0:T(8,128)S(1)} %bitcast.9, f32[128,1536]{1,0:T(8,128)S(1)} %collective-permute-done.4.far_ref), custom_call_target="tpu_custom_call" | custom-call | tf_op jit(solution)/shard_map/factored/pallas_call | solution.py:217
  97.0 3.1 %fusion.2 = f32[2048,256]{1,0:T(8,128)} fusion(f32[2048,256]{1,0:T(8,128)S(1)} %fusion.sample_ref, f32[256,256]{1,0:T(8,128)S(1)} %get-tuple-element.8), kind=kOutput, calls=%fused_computation.2 | convolution fusion | flops 1610612736 | bytes 4456448 | tf_op jit(solution)/shard_map/dot_general | solution.py:23
  (2 shorter events, 0.0 us)
Async XLA Ops:
  0.6 1.2 %copy-start = (f32[1024,256]{1,0:T(8,128)S(1)}, f32[1024,256]{1,0:T(8,128)}, u32[]{:S(2)}) copy-start(f32[1024,256]{1,0:T(8,128)} %param.3) | copy-start | bytes 3145732
  1.9 10.0 %copy-start.1 = (f32[2048,1024]{1,0:T(8,128)S(1)}, f32[2048,1024]{1,0:T(8,128)}, u32[]{:S(2)}) copy-start(f32[2048,1024]{1,0:T(8,128)} %param.2) | copy-start | bytes 25165828
  19.6 5.2 %collective-permute-start = (f32[128,1536]{1,0:T(8,128)S(1)}, f32[128,1536]{1,0:T(8,128)S(1)}, u32[]{:S(2)}, u32[]{:S(2)}) collective-permute-start(f32[128,1536]{1,0:T(8,128)S(1)} %get-tuple-element.7), channel_id=1, source_target_pairs={{0,8},{8,0},{1,9},{9,1},{2,10},{10,2},{3,11},{11,3},{4,12},{12,4},... | collective-permute-start | bytes 2359304 | tf_op jit(solution)/shard_map/ppermute | solution.py:242
  43.1 3.4 %collective-permute-start.1 = (f32[8,1536]{1,0:T(8,128)S(1)}, f32[8,1536]{1,0:T(8,128)S(1)}, u32[]{:S(2)}, u32[]{:S(2)}) collective-permute-start(f32[8,1536]{1,0:T(8,128)S(1)} %stack_sum.1.a_ref), channel_id=1, source_target_pairs={{0,1},{1,0},{2,3},{3,2},{4,5},{5,4},{6,7},{7,6},{8,9},{9,8},{10,11... | collective-permute-start | bytes 147464 | tf_op jit(solution)/shard_map/ppermute | solution.py:246
  46.5 4.6 %collective-permute-start.2 = (f32[8,1536]{1,0:T(8,128)S(1)}, f32[8,1536]{1,0:T(8,128)S(1)}, u32[]{:S(2)}, u32[]{:S(2)}) collective-permute-start(f32[8,1536]{1,0:T(8,128)S(1)} %pair_sum.5.a_ref), channel_id=1, source_target_pairs={{0,2},{1,3},{2,0},{3,1},{4,6},{5,7},{6,4},{7,5},{8,10},{9,11},{10,... | collective-permute-start | bytes 147464 | tf_op jit(solution)/shard_map/ppermute | solution.py:246
  51.1 7.8 %collective-permute-start.3 = (f32[8,1536]{1,0:T(8,128)S(1)}, f32[8,1536]{1,0:T(8,128)S(1)}, u32[]{:S(2)}, u32[]{:S(2)}) collective-permute-start(f32[8,1536]{1,0:T(8,128)S(1)} %pair_sum.6.a_ref), channel_id=1, source_target_pairs={{0,4},{1,5},{2,6},{3,7},{4,0},{5,1},{6,2},{7,3},{8,12},{9,13},{10,... | collective-permute-start | bytes 147464 | tf_op jit(solution)/shard_map/ppermute | solution.py:246
  72.8 8.2 %collective-permute-start.4 = (f32[128,1536]{1,0:T(8,128)S(1)}, f32[128,1536]{1,0:T(8,128)S(1)}, u32[]{:S(2)}, u32[]{:S(2)}) collective-permute-start(f32[128,1536]{1,0:T(8,128)S(1)} %bitcast.8), channel_id=1, source_target_pairs={{0,8},{8,0},{1,9},{9,1},{2,10},{10,2},{3,11},{11,3},{4,12},{12,4},... | collective-permute-start | bytes 2359304 | tf_op jit(solution)/shard_map/ppermute | solution.py:251

commit v3 on v2

--- a/solution.py
+++ b/solution.py
@@ -16,7 +16,9 @@
 HI = lax.Precision.HIGHEST
 F32 = jnp.float32
 BF16 = jnp.bfloat16
-BLOCK = 64
+BLOCK = 128
+GRAM = 384
+WIDTH = GRAM + 1024
 
 
 def dot(a, b, dims=((1,), (0,)), precision=HI):
@@ -71,13 +73,16 @@
     h, l = half_gram(sample_ref, top, 1024)
     hi, e = two_sum(h, h.T)
     hi, lo = two_sum(hi, (l + l.T) + e)
-    x_ref[:, :256] = hi
-    x_ref[:, 256:] = lo
+    for i in range(2):
+        at, mid = 128 * i, 128 + 64 * i
+        x_ref[i, :, :128] = hi[at : at + 128, at : at + 128]
+        x_ref[i, :, 128:256] = lo[at : at + 128, at : at + 128]
+        x_ref[i, :, 256:320] = hi[:128, mid : mid + 64]
+        x_ref[i, :, 320:] = lo[:128, mid : mid + 64]
     core = lax.axis_index(CORE)
     for half, ref in ((core, mine_ref), (1 - core, other_ref)):
-        at = pl.multiple_of(half * 128, 128)
-        ref[:, :512] = x_ref[pl.ds(at, 128), :]
-        ref[:, 512:] = terms_ref[pl.ds(at, 128), :]
+        ref[:, :GRAM] = x_ref[half]
+        ref[:, GRAM:] = terms_ref[pl.ds(pl.multiple_of(half * 128, 128), 128), :]
 
 
 def local_halves(sample, terms):
@@ -85,17 +90,20 @@
         gram_kernel,
         in_specs=in_vmem(2),
         out_specs=in_vmem(2),
-        out_shape=[jax.ShapeDtypeStruct((128, 1536), F32)] * 2,
-        scratch_shapes=[pltpu.VMEM((256, 512), F32)],
+        out_shape=[jax.ShapeDtypeStruct((128, WIDTH), F32)] * 2,
+        scratch_shapes=[pltpu.VMEM((2, 128, GRAM), F32)],
         compiler_params=pltpu.CompilerParams(vmem_limit_bytes=20 * 2**20),
         name="local_halves",
     )(sample, terms)
 
 
 def plus(a, b):
-    hi, e = two_sum(a[:, :256], b[:, :256])
-    hi, lo = two_sum(hi, (a[:, 256:512] + b[:, 256:512]) + e)
-    return jnp.concatenate([hi, lo, a[:, 512:] + b[:, 512:]], axis=1)
+    out = []
+    for at, w in ((0, 128), (256, 64)):
+        hi, e = two_sum(a[:, at : at + w], b[:, at : at + w])
+        low = slice(at + w, at + 2 * w)
+        out += two_sum(hi, (a[:, low] + b[:, low]) + e)
+    return jnp.concatenate([*out, a[:, GRAM:] + b[:, GRAM:]], axis=1)
 
 
 def pair_kernel(a_ref, b_ref, out_ref):
@@ -137,24 +145,34 @@
         across = lambda x, j: jnp.broadcast_to(x[:, 8 * t + j : 8 * t + j + 1], shape)
         u = [jnp.broadcast_to(tiles[t][i : i + 1, :], shape) for i in range(8)]
         s = {(i, j): across(u[i], j) for i in range(8) for j in range(i, 8)}
-        below = {v: [across(tiles[v], k) for k in range(8)] for v in range(t + 1, nt)}
-        l = {}
+        near = {v: [across(tiles[v], k) for k in range(8)] for v in range(t + 1, min(t + 2, nt))}
+        l, scale = {}, []
         for k in range(8):
             rho = lax.rsqrt(s[k, k])
+            scale.append(rho)
             for i in range(k + 1, 8):
-                l[i] = s[k, i] * rho
+                l[i, k] = s[k, i] * rho
             for i in range(k + 1, 8):
                 for j in range(i, 8):
-                    s[i, j] = s[i, j] - l[i] * l[j]
-            for w in [u, *below.values()]:
+                    s[i, j] = s[i, j] - l[i, k] * l[j, k]
+            for w in [u, *near.values()]:
                 w[k] = w[k] * rho
                 for i in range(k + 1, 8):
-                    w[i] = w[i] - l[i] * w[k]
+                    w[i] = w[i] - l[i, k] * w[k]
         out = u[0]
         for k in range(1, 8):
             out = jnp.where(sub == k, u[k], out)
-        for v, w in below.items():
-            p = [w[k] * u[k] for k in range(8)]
+        z = list(u)
+        if t + 2 < nt:
+            for k in range(7, -1, -1):
+                z[k] = z[k] * scale[k]
+                for i in range(k):
+                    z[i] = z[i] - l[k, i] * z[k]
+        for v in range(t + 1, nt):
+            if v in near:
+                p = [near[v][k] * u[k] for k in range(8)]
+            else:
+                p = [across(tiles[v], k) * z[k] for k in range(8)]
             while len(p) > 1:
                 p = [p[i] + p[i + 1] for i in range(0, len(p), 2)]
             tiles[v] = tiles[v] - p[0]
@@ -162,13 +180,19 @@
     return jnp.concatenate(tiles, axis=0)[:, b:]
 
 
-def factor_kernel(root, near_ref, far_ref, inverse_ref, projection_ref, g_ref, w_ref, r_ref, y_ref, a_ref, m_ref, u_ref):
+def factor_kernel(root, near_ref, far_ref, inverse_ref, projection_ref, x_ref, g_ref, w_ref, r_ref, y_ref, a_ref, m_ref, u_ref):
     n = 256
     core = lax.axis_index(CORE)
     for ref, half in ((near_ref, core), (far_ref, 1 - core)):
-        at = pl.multiple_of(half * 128, 128)
-        g_ref[pl.ds(at, 128), :] = ref[:, :512]
-        w_ref[pl.ds(at, 128), :] = ref[:, 512:]
+        x_ref[half] = ref[:, :GRAM]
+        w_ref[pl.ds(pl.multiple_of(half * 128, 128), 128), :] = ref[:, GRAM:]
+    for at in (0, 1):
+        corner = [x_ref[i, :, 128 * at : 128 * at + 128] for i in (0, 1)]
+        side = jnp.concatenate([x_ref[i, :, 256 + 64 * at : 320 + 64 * at] for i in (0, 1)], axis=1)
+        g_ref[:128, n * at : n * at + 128] = corner[0]
+        g_ref[:128, n * at + 128 : n * at + n] = side
+        g_ref[128:, n * at : n * at + 128] = side.T
+        g_ref[128:, n * at + 128 : n * at + n] = corner[1]
     row, col = (lax.broadcasted_iota(jnp.int32, (n, n), i) for i in (0, 1))
     eye = (row == col).astype(F32)
     lower = jnp.where(row > col, 1.0, jnp.where(row == col, 0.5, 0.0))
@@ -220,7 +244,7 @@
         out_specs=in_vmem(2),
         out_shape=[jax.ShapeDtypeStruct((n, n), F32), jax.ShapeDtypeStruct((n, 1024), F32)],
         scratch_shapes=[
-            pltpu.VMEM(s, F32) for s in ((n, 512), (n, 1024), (n, n), (n, n), (n, 512), (n, n), (n, n))
+            pltpu.VMEM(s, F32) for s in ((2, 128, GRAM), (n, 512), (n, 1024), (n, n), (n, n), (n, 512), (n, n), (n, n))
         ],
         compiler_params=pltpu.CompilerParams(vmem_limit_bytes=16 * 2**20),
         name="factored",
@@ -240,14 +264,15 @@
     terms = dot(sample, corpus, ((0,), (0,)), lax.Precision.HIGH)
     mine, other = local_halves(sample, terms)
     own = added(pair_kernel, mine.shape, "pair_sum", mine, lax.ppermute(other, CORE, swap))
-    whole = added(stack_kernel, (8, 1536), "stack_sum", exchanged(own.reshape(plane, 8, 1536), PLANE))
-    far = 1
-    while far < line:
-        arrived = lax.ppermute(whole, LINE, [(i, i ^ far) for i in range(line)])
-        far *= 2
-        out = (8, 1536) if far < line else (plane, 8, 1536)
+    whole = added(stack_kernel, (8, WIDTH), "stack_sum", exchanged(own.reshape(plane, 8, WIDTH), PLANE))
+    reach = 1
+    while reach < line:
+        flip = reach if 2 * reach < line else line - 1
+        arrived = lax.ppermute(whole, LINE, [(i, i ^ flip) for i in range(line)])
+        reach *= 2
+        out = (8, WIDTH) if reach < line else (plane, 8, WIDTH)
         whole = added(pair_kernel, out, "pair_sum", whole, arrived)
-    near = exchanged(whole, PLANE).reshape(128, 1536)
+    near = exchanged(whole, PLANE).reshape(128, WIDTH)
     far = lax.ppermute(near, CORE, swap)
     inverse, projection = factored(near, far, root)
     basis = dot(sample, inverse)

time: 100 us -> 98.3 us (0.983)
  starting transfers between devices: 20.8 us -> 18.8 us
  Pallas kernels: 19.8 us -> 21.6 us
  blocking collectives: 32 us -> 30.7 us
    pallas_call x5, Pallas kernels: 0.27 us -> 2.83 us  [added(): pl.pallas_call(kernel, in_specs=in_vmem(len(parts)), out_specs=in_vmem(1)...]
    ppermute x3, starting transfers between devices: 11.2 us -> 9.42 us  [on_device(): arrived = lax.ppermute(whole, LINE, [(i, i ^ flip) for i in range(line)])]
    all_to_all x2, blocking collectives: 32 us -> 30.7 us  [exchanged(): return lax.all_to_all(x, axis, 0, 0, tiled=True)]
where the time goes in v3:
time: 98.3 us; the launch traced here: 98.2 us
  blocking collectives  30.7 us (31%)
  Pallas kernels  21.6 us (22%)
  starting transfers between devices  18.8 us (19%)
  matrix products  17.2 us (17%)
  waiting for transfers between devices  7.95 us (8%)
  local copies, waits for them, and re-layouts  1.23 us (1%)
    all_to_all x2, blocking collectives, exchanged(): return lax.all_to_all(x, axis, 0, 0, tiled=True)  30.7 us
    dot_general x3, matrix products, dot(): lax.dot_general(a, b, (dims, ((), ())), precision=precision, preferred_el...  17.2 us
    pallas_call x1, Pallas kernels, factored(): pl.pallas_call(functools.partial(factor_kernel, root), in_specs=in_vmem(2...  15.3 us
    ppermute x3, starting transfers between devices, on_device(): arrived = lax.ppermute(whole, LINE, [(i, i ^ flip) for i in range(line)])  9.42 us
    ppermute x1, starting transfers between devices, on_device(): far = lax.ppermute(near, CORE, swap)  6.07 us
    ppermute x3, waiting for transfers between devices, on_device(): arrived = lax.ppermute(whole, LINE, [(i, i ^ flip) for i in range(line)])  4.31 us
    pallas_call x1, Pallas kernels, local_halves(): pl.pallas_call(gram_kernel, in_specs=in_vmem(2), out_specs=in_vmem(2), ou...  3.48 us
    ppermute x1, starting transfers between devices, on_device(): lax.ppermute(other, CORE, swap)  3.29 us
  transfers between devices with their start and end apart: 5, of which 5 were waited for; matrix products, arithmetic and copies ran while one was open for 0% of the time, Pallas kernels for 0%

profile of v3, /device:TPU:1, one launch (start us, length us, event | category | flops | bytes accessed | tf_op | source)
XLA Modules:
  0.0 98.2 jit_solution(10634771938440899004)
XLA Ops:
  0.6 0.0 copy-start
  0.6 1.2 %copy-done = f32[1024,256]{1,0:T(8,128)S(1)} copy-done((f32[1024,256]{1,0:T(8,128)S(1)}, f32[1024,256]{1,0:T(8,128)}, u32[]{:S(2)}) %copy-start) | copy-done | bytes 1048600
  1.9 0.0 copy-start.1
  1.9 9.9 %fusion.sample_ref = f32[2048,256]{1,0:T(8,128)S(1)} fusion(f32[2048,1024]{1,0:T(8,128)} %param.2, f32[1024,256]{1,0:T(8,128)S(1)} %copy-done), kind=kOutput, calls=%fused_computation | convolution fusion | flops 6442450944 | bytes 11534336 | tf_op jit(solution)/shard_map/dot_general | solution.py:25
  11.8 0.0 copy-done.1
  11.8 4.2 %fusion.1.terms_ref = f32[256,1024]{1,0:T(8,128)S(1)} fusion(f32[2048,256]{1,0:T(8,128)S(1)} %fusion.sample_ref, f32[2048,1024]{1,0:T(8,128)S(1)} %copy-done.1), kind=kOutput, calls=%fused_computation.1 | convolution fusion | flops 3221225472 | bytes 11534336 | tf_op jit(solution)/shard_map/dot_general | solution.py:25
  16.0 3.5 %local_halves.1 = (f32[128,1408]{1,0:T(8,128)S(1)}, f32[128,1408]{1,0:T(8,128)S(1)}) custom-call(f32[2048,256]{1,0:T(8,128)S(1)} %fusion.sample_ref, f32[256,1024]{1,0:T(8,128)S(1)} %fusion.1.terms_ref), custom_call_target="tpu_custom_call" | custom-call | tf_op jit(solution)/shard_map/local_halves/pallas_call | solution.py:89
  19.5 3.3 %collective-permute-start = (f32[128,1408]{1,0:T(8,128)S(1)}, f32[128,1408]{1,0:T(8,128)S(1)}, u32[]{:S(2)}, u32[]{:S(2)}) collective-permute-start(f32[128,1408]{1,0:T(8,128)S(1)} %get-tuple-element.7), channel_id=1, source_target_pairs={{0,8},{8,0},{1,9},{9,1},{2,10},{10,2},{3,11},{11,3},{4,12},{12,4},... | collective-permute-start | bytes 2162696 | tf_op jit(solution)/shard_map/ppermute | solution.py:266
  22.8 1.8 %collective-permute-done.b_ref = f32[128,1408]{1,0:T(8,128)S(1)} collective-permute-done((f32[128,1408]{1,0:T(8,128)S(1)}, f32[128,1408]{1,0:T(8,128)S(1)}, u32[]{:S(2)}, u32[]{:S(2)}) %collective-permute-start) | collective-permute-done | bytes 720928 | tf_op jit(solution)/shard_map/ppermute | solution.py:266
  24.6 0.4 pair_sum.4
  25.0 17.4 %all_to_all.10.x_ref = f32[16,8,1408]{2,1,0:T(8,128)S(1)} all-to-all(f32[16,8,1408]{2,1,0:T(8,128)S(1)} %bitcast.10), channel_id=1, replica_groups=mesh['wide_0'=4,'wide_1'=4,'wide_2'=2,'narrow'=8] {'wide_0','wide_1'}, dimensions={0} | all-to-all | bytes 1441792 | tf_op jit(solution)/shard_map/all_to_all | solution.py:255
  42.3 1.4 %stack_sum.1.a_ref = f32[8,1408]{1,0:T(8,128)S(1)} custom-call(f32[16,8,1408]{2,1,0:T(8,128)S(1)} %all_to_all.10.x_ref), custom_call_target="tpu_custom_call" | custom-call | tf_op jit(solution)/shard_map/stack_sum/pallas_call | solution.py:126
  43.7 1.6 %collective-permute-start.1 = (f32[8,1408]{1,0:T(8,128)S(1)}, f32[8,1408]{1,0:T(8,128)S(1)}, u32[]{:S(2)}, u32[]{:S(2)}) collective-permute-start(f32[8,1408]{1,0:T(8,128)S(1)} %stack_sum.1.a_ref), channel_id=1, source_target_pairs={{0,1},{1,0},{2,3},{3,2},{4,5},{5,4},{6,7},{7,6},{8,9},{9,8},{10,11... | collective-permute-start | bytes 135176 | tf_op jit(solution)/shard_map/ppermute | solution.py:271
  45.4 1.4 %collective-permute-done.1.b_ref = f32[8,1408]{1,0:T(8,128)S(1)} collective-permute-done((f32[8,1408]{1,0:T(8,128)S(1)}, f32[8,1408]{1,0:T(8,128)S(1)}, u32[]{:S(2)}, u32[]{:S(2)}) %collective-permute-start.1) | collective-permute-done | bytes 45088 | tf_op jit(solution)/shard_map/ppermute | solution.py:271
  46.8 0.4 pair_sum.5.a_ref
  47.2 3.0 %collective-permute-start.2 = (f32[8,1408]{1,0:T(8,128)S(1)}, f32[8,1408]{1,0:T(8,128)S(1)}, u32[]{:S(2)}, u32[]{:S(2)}) collective-permute-start(f32[8,1408]{1,0:T(8,128)S(1)} %pair_sum.5.a_ref), channel_id=1, source_target_pairs={{0,2},{1,3},{2,0},{3,1},{4,6},{5,7},{6,4},{7,5},{8,10},{9,11},{10,... | collective-permute-start | bytes 135176 | tf_op jit(solution)/shard_map/ppermute | solution.py:271
  50.1 1.4 %collective-permute-done.2.b_ref = f32[8,1408]{1,0:T(8,128)S(1)} collective-permute-done((f32[8,1408]{1,0:T(8,128)S(1)}, f32[8,1408]{1,0:T(8,128)S(1)}, u32[]{:S(2)}, u32[]{:S(2)}) %collective-permute-start.2) | collective-permute-done | bytes 45088 | tf_op jit(solution)/shard_map/ppermute | solution.py:271
  51.6 0.4 pair_sum.6.a_ref
  51.9 4.8 %collective-permute-start.3 = (f32[8,1408]{1,0:T(8,128)S(1)}, f32[8,1408]{1,0:T(8,128)S(1)}, u32[]{:S(2)}, u32[]{:S(2)}) collective-permute-start(f32[8,1408]{1,0:T(8,128)S(1)} %pair_sum.6.a_ref), channel_id=1, source_target_pairs={{0,7},{1,6},{2,5},{3,4},{4,3},{5,2},{6,1},{7,0},{8,15},{9,14},{10,... | collective-permute-start | bytes 135176 | tf_op jit(solution)/shard_map/ppermute | solution.py:271
  56.7 1.4 %collective-permute-done.3.b_ref = f32[8,1408]{1,0:T(8,128)S(1)} collective-permute-done((f32[8,1408]{1,0:T(8,128)S(1)}, f32[8,1408]{1,0:T(8,128)S(1)}, u32[]{:S(2)}, u32[]{:S(2)}) %collective-permute-start.3) | collective-permute-done | bytes 45088 | tf_op jit(solution)/shard_map/ppermute | solution.py:271
  58.2 0.4 pair_sum.7
  58.5 13.4 %all_to_all.11 = f32[16,8,1408]{2,1,0:T(8,128)S(1)} all-to-all(f32[16,8,1408]{2,1,0:T(8,128)S(1)} %pair_sum.7), channel_id=1, replica_groups=mesh['wide_0'=4,'wide_1'=4,'wide_2'=2,'narrow'=8] {'wide_0','wide_1'}, dimensions={0} | all-to-all | bytes 1441792 | tf_op jit(solution)/shard_map/all_to_all | solution.py:255
  71.9 6.1 %collective-permute-start.4 = (f32[128,1408]{1,0:T(8,128)S(1)}, f32[128,1408]{1,0:T(8,128)S(1)}, u32[]{:S(2)}, u32[]{:S(2)}) collective-permute-start(f32[128,1408]{1,0:T(8,128)S(1)} %bitcast.8), channel_id=1, source_target_pairs={{0,8},{8,0},{1,9},{9,1},{2,10},{10,2},{3,11},{11,3},{4,12},{12,4},... | collective-permute-start | bytes 2162696 | tf_op jit(solution)/shard_map/ppermute | solution.py:276
  77.9 1.8 %collective-permute-done.4.far_ref = f32[128,1408]{1,0:T(8,128)S(1)} collective-permute-done((f32[128,1408]{1,0:T(8,128)S(1)}, f32[128,1408]{1,0:T(8,128)S(1)}, u32[]{:S(2)}, u32[]{:S(2)}) %collective-permute-start.4) | collective-permute-done | bytes 720928 | tf_op jit(solution)/shard_map/ppermute | solution.py:276
  79.8 15.3 %factored.1 = (f32[256,256]{1,0:T(8,128)S(1)}, f32[256,1024]{1,0:T(8,128)}) custom-call(f32[128,1408]{1,0:T(8,128)S(1)} %bitcast.9, f32[128,1408]{1,0:T(8,128)S(1)} %collective-permute-done.4.far_ref), custom_call_target="tpu_custom_call" | custom-call | tf_op jit(solution)/shard_map/factored/pallas_call | solution.py:241
  95.0 3.1 %fusion.2 = f32[2048,256]{1,0:T(8,128)} fusion(f32[2048,256]{1,0:T(8,128)S(1)} %fusion.sample_ref, f32[256,256]{1,0:T(8,128)S(1)} %get-tuple-element.8), kind=kOutput, calls=%fused_computation.2 | convolution fusion | flops 1610612736 | bytes 4456448 | tf_op jit(solution)/shard_map/dot_general | solution.py:25
Async XLA Ops:
  0.6 1.2 %copy-start = (f32[1024,256]{1,0:T(8,128)S(1)}, f32[1024,256]{1,0:T(8,128)}, u32[]{:S(2)}) copy-start(f32[1024,256]{1,0:T(8,128)} %param.3) | copy-start | bytes 3145732
  1.9 10.0 %copy-start.1 = (f32[2048,1024]{1,0:T(8,128)S(1)}, f32[2048,1024]{1,0:T(8,128)}, u32[]{:S(2)}) copy-start(f32[2048,1024]{1,0:T(8,128)} %param.2) | copy-start | bytes 25165828
  19.5 5.1 %collective-permute-start = (f32[128,1408]{1,0:T(8,128)S(1)}, f32[128,1408]{1,0:T(8,128)S(1)}, u32[]{:S(2)}, u32[]{:S(2)}) collective-permute-start(f32[128,1408]{1,0:T(8,128)S(1)} %get-tuple-element.7), channel_id=1, source_target_pairs={{0,8},{8,0},{1,9},{9,1},{2,10},{10,2},{3,11},{11,3},{4,12},{12,4},... | collective-permute-start | bytes 2162696 | tf_op jit(solution)/shard_map/ppermute | solution.py:266
  43.7 3.1 %collective-permute-start.1 = (f32[8,1408]{1,0:T(8,128)S(1)}, f32[8,1408]{1,0:T(8,128)S(1)}, u32[]{:S(2)}, u32[]{:S(2)}) collective-permute-start(f32[8,1408]{1,0:T(8,128)S(1)} %stack_sum.1.a_ref), channel_id=1, source_target_pairs={{0,1},{1,0},{2,3},{3,2},{4,5},{5,4},{6,7},{7,6},{8,9},{9,8},{10,11... | collective-permute-start | bytes 135176 | tf_op jit(solution)/shard_map/ppermute | solution.py:271
  47.2 4.4 %collective-permute-start.2 = (f32[8,1408]{1,0:T(8,128)S(1)}, f32[8,1408]{1,0:T(8,128)S(1)}, u32[]{:S(2)}, u32[]{:S(2)}) collective-permute-start(f32[8,1408]{1,0:T(8,128)S(1)} %pair_sum.5.a_ref), channel_id=1, source_target_pairs={{0,2},{1,3},{2,0},{3,1},{4,6},{5,7},{6,4},{7,5},{8,10},{9,11},{10,... | collective-permute-start | bytes 135176 | tf_op jit(solution)/shard_map/ppermute | solution.py:271
  51.9 6.2 %collective-permute-start.3 = (f32[8,1408]{1,0:T(8,128)S(1)}, f32[8,1408]{1,0:T(8,128)S(1)}, u32[]{:S(2)}, u32[]{:S(2)}) collective-permute-start(f32[8,1408]{1,0:T(8,128)S(1)} %pair_sum.6.a_ref), channel_id=1, source_target_pairs={{0,7},{1,6},{2,5},{3,4},{4,3},{5,2},{6,1},{7,0},{8,15},{9,14},{10,... | collective-permute-start | bytes 135176 | tf_op jit(solution)/shard_map/ppermute | solution.py:271
  71.9 7.9 %collective-permute-start.4 = (f32[128,1408]{1,0:T(8,128)S(1)}, f32[128,1408]{1,0:T(8,128)S(1)}, u32[]{:S(2)}, u32[]{:S(2)}) collective-permute-start(f32[128,1408]{1,0:T(8,128)S(1)} %bitcast.8), channel_id=1, source_target_pairs={{0,8},{8,0},{1,9},{9,1},{2,10},{10,2},{3,11},{11,3},{4,12},{12,4},... | collective-permute-start | bytes 2162696 | tf_op jit(solution)/shard_map/ppermute | solution.py:276

commit v4 on v3

--- a/solution.py
+++ b/solution.py
@@ -14,6 +14,7 @@
 CORE = "wide_2"
 LINE = "narrow"
 HI = lax.Precision.HIGHEST
+MID = lax.Precision.HIGH
 F32 = jnp.float32
 BF16 = jnp.bfloat16
 BLOCK = 128
@@ -97,29 +98,46 @@
     )(sample, terms)
 
 
-def plus(a, b):
-    out = []
-    for at, w in ((0, 128), (256, 64)):
-        hi, e = two_sum(a[:, at : at + w], b[:, at : at + w])
-        low = slice(at + w, at + 2 * w)
-        out += two_sum(hi, (a[:, low] + b[:, low]) + e)
-    return jnp.concatenate([*out, a[:, GRAM:] + b[:, GRAM:]], axis=1)
+def total(parts):
+    def compensated(x):
+        error = 0.0
+        while len(x) > 1:
+            pairs = [two_sum(x[i], x[i + 1]) for i in range(0, len(x), 2)]
+            error = error + functools.reduce(jnp.add, [e for _, e in pairs])
+            x = [s for s, _ in pairs]
+        return x[0], error
+
+    def plain(x):
+        while len(x) > 1:
+            x = [x[i] + x[i + 1] for i in range(0, len(x), 2)]
+        return x[0]
+
+    hi, e = compensated([p[:, :128] for p in parts])
+    lo = plain([p[:, 128:256] for p in parts]) + e
+    mixed, e = compensated([p[:, 256:GRAM] for p in parts])
+    lane = lax.broadcasted_iota(jnp.int32, mixed.shape, 1)
+    mixed = jnp.where(lane < 64, mixed, mixed + pltpu.roll(e, 64, 1))
+    return hi, lo, mixed, plain([p[:, GRAM:] for p in parts])
+
+
+def store(ref, parts):
+    at = 0
+    for x in parts:
+        ref[:, at : at + x.shape[1]] = x
+        at += x.shape[1]
 
 
 def pair_kernel(a_ref, b_ref, out_ref):
-    s = plus(a_ref[...], b_ref[...])
+    s = total([a_ref[...], b_ref[...]])
     if len(out_ref.shape) == 2:
-        out_ref[...] = s
+        store(out_ref, s)
     else:
         for i in range(out_ref.shape[0]):
-            out_ref[i] = s
+            store(out_ref.at[i], s)
 
 
 def stack_kernel(x_ref, out_ref):
-    parts = [x_ref[i] for i in range(x_ref.shape[0])]
-    while len(parts) > 1:
-        parts = [plus(parts[i], parts[i + 1]) for i in range(0, len(parts), 2)]
-    out_ref[...] = parts[0]
+    store(out_ref, total([x_ref[i] for i in range(x_ref.shape[0])]))
 
 
 def added(kernel, shape, name, *parts):
@@ -219,7 +237,7 @@
     d = d + ((g_ref[:, n:] - fine) + (e1 + e2))
 
     f = dot(r, y, nt) - eye
-    m = eye + ((f + f.T) + dot(f, f, tn) + dot(dot(y, d), y, nt))
+    m = eye + ((f + f.T) + dot(f, f, tn, MID) + dot(dot(y, d, precision=MID), y, nt, MID))
     m_ref[...] = m
     u_ref[...] = eye - lower * (m - eye)
 
@@ -227,7 +245,7 @@
         count, _ = carry
         u = u_ref[...]
         off = dot(dot(u, m_ref[...]), u, nt) - eye
-        u_ref[...] = u - dot(lower * off, u)
+        u_ref[...] = u - dot(lower * off, u, precision=MID)
         return count + 1, jnp.max(jnp.abs(off))
 
     lax.while_loop(lambda c: (c[0] < 24) & (c[1] > 1e-4), refine, (0, jnp.float32(1.0)))
@@ -261,7 +279,7 @@
     root = math.sqrt(total_rows)
     swap = [(0, 1), (1, 0)]
     sample = dot(corpus, sketch)
-    terms = dot(sample, corpus, ((0,), (0,)), lax.Precision.HIGH)
+    terms = dot(sample, corpus, ((0,), (0,)), MID)
     mine, other = local_halves(sample, terms)
     own = added(pair_kernel, mine.shape, "pair_sum", mine, lax.ppermute(other, CORE, swap))
     whole = added(stack_kernel, (8, WIDTH), "stack_sum", exchanged(own.reshape(plane, 8, WIDTH), PLANE))

time: 98.3 us -> 95.7 us (0.974)
  Pallas kernels: 21.6 us -> 18.7 us
    pallas_call x5, Pallas kernels: 2.83 us -> 0.5 us  [added(): pl.pallas_call(kernel, in_specs=in_vmem(len(parts)), out_specs=in_vmem(1)...]
where the time goes in v4:
time: 95.7 us; the launch traced here: 95.5 us
  blocking collectives  30.7 us (32%)
  starting transfers between devices  19 us (20%)
  Pallas kernels  18.7 us (20%)
  matrix products  17.2 us (18%)
  waiting for transfers between devices  7.96 us (8%)
  local copies, waits for them, and re-layouts  1.23 us (1%)
    all_to_all x2, blocking collectives, exchanged(): return lax.all_to_all(x, axis, 0, 0, tiled=True)  30.7 us
    dot_general x3, matrix products, dot(): lax.dot_general(a, b, (dims, ((), ())), precision=precision, preferred_el...  17.2 us
    pallas_call x1, Pallas kernels, factored(): pl.pallas_call(functools.partial(factor_kernel, root), in_specs=in_vmem(2...  14.7 us
    ppermute x3, starting transfers between devices, on_device(): arrived = lax.ppermute(whole, LINE, [(i, i ^ flip) for i in range(line)])  9.68 us
    ppermute x1, starting transfers between devices, on_device(): far = lax.ppermute(near, CORE, swap)  6.07 us
    ppermute x3, waiting for transfers between devices, on_device(): arrived = lax.ppermute(whole, LINE, [(i, i ^ flip) for i in range(line)])  4.32 us
    pallas_call x1, Pallas kernels, local_halves(): pl.pallas_call(gram_kernel, in_specs=in_vmem(2), out_specs=in_vmem(2), ou...  3.48 us
    ppermute x1, starting transfers between devices, on_device(): lax.ppermute(other, CORE, swap)  3.29 us
  transfers between devices with their start and end apart: 5, of which 5 were waited for; matrix products, arithmetic and copies ran while one was open for 0% of the time, Pallas kernels for 0%

profile of v4, /device:TPU:1, one launch (start us, length us, event | category | flops | bytes accessed | tf_op | source)
XLA Modules:
  0.0 95.5 jit_solution(6875481512304761413)
XLA Ops:
  0.6 0.0 copy-start
  0.6 1.2 %copy-done = f32[1024,256]{1,0:T(8,128)S(1)} copy-done((f32[1024,256]{1,0:T(8,128)S(1)}, f32[1024,256]{1,0:T(8,128)}, u32[]{:S(2)}) %copy-start) | copy-done | bytes 1048600
  1.9 0.0 copy-start.1
  1.9 9.9 %fusion.sample_ref = f32[2048,256]{1,0:T(8,128)S(1)} fusion(f32[2048,1024]{1,0:T(8,128)} %param.2, f32[1024,256]{1,0:T(8,128)S(1)} %copy-done), kind=kOutput, calls=%fused_computation | convolution fusion | flops 6442450944 | bytes 11534336 | tf_op jit(solution)/shard_map/dot_general | solution.py:26
  11.8 0.0 copy-done.1
  11.8 4.2 %fusion.1.terms_ref = f32[256,1024]{1,0:T(8,128)S(1)} fusion(f32[2048,256]{1,0:T(8,128)S(1)} %fusion.sample_ref, f32[2048,1024]{1,0:T(8,128)S(1)} %copy-done.1), kind=kOutput, calls=%fused_computation.1 | convolution fusion | flops 3221225472 | bytes 11534336 | tf_op jit(solution)/shard_map/dot_general | solution.py:26
  16.0 3.5 %local_halves.1 = (f32[128,1408]{1,0:T(8,128)S(1)}, f32[128,1408]{1,0:T(8,128)S(1)}) custom-call(f32[2048,256]{1,0:T(8,128)S(1)} %fusion.sample_ref, f32[256,1024]{1,0:T(8,128)S(1)} %fusion.1.terms_ref), custom_call_target="tpu_custom_call" | custom-call | tf_op jit(solution)/shard_map/local_halves/pallas_call | solution.py:90
  19.5 3.3 %collective-permute-start = (f32[128,1408]{1,0:T(8,128)S(1)}, f32[128,1408]{1,0:T(8,128)S(1)}, u32[]{:S(2)}, u32[]{:S(2)}) collective-permute-start(f32[128,1408]{1,0:T(8,128)S(1)} %get-tuple-element.7), channel_id=1, source_target_pairs={{0,8},{8,0},{1,9},{9,1},{2,10},{10,2},{3,11},{11,3},{4,12},{12,4},... | collective-permute-start | bytes 2162696 | tf_op jit(solution)/shard_map/ppermute | solution.py:284
  22.8 1.8 %collective-permute-done.b_ref = f32[128,1408]{1,0:T(8,128)S(1)} collective-permute-done((f32[128,1408]{1,0:T(8,128)S(1)}, f32[128,1408]{1,0:T(8,128)S(1)}, u32[]{:S(2)}, u32[]{:S(2)}) %collective-permute-start) | collective-permute-done | bytes 720928 | tf_op jit(solution)/shard_map/ppermute | solution.py:284
  24.6 0.2 pair_sum.4
  24.7 17.4 %all_to_all.10.x_ref = f32[16,8,1408]{2,1,0:T(8,128)S(1)} all-to-all(f32[16,8,1408]{2,1,0:T(8,128)S(1)} %bitcast.10), channel_id=1, replica_groups=mesh['wide_0'=4,'wide_1'=4,'wide_2'=2,'narrow'=8] {'wide_0','wide_1'}, dimensions={0} | all-to-all | bytes 1441792 | tf_op jit(solution)/shard_map/all_to_all | solution.py:273
  42.1 0.1 stack_sum.1.a_ref
  42.2 1.9 %collective-permute-start.1 = (f32[8,1408]{1,0:T(8,128)S(1)}, f32[8,1408]{1,0:T(8,128)S(1)}, u32[]{:S(2)}, u32[]{:S(2)}) collective-permute-start(f32[8,1408]{1,0:T(8,128)S(1)} %stack_sum.1.a_ref), channel_id=1, source_target_pairs={{0,1},{1,0},{2,3},{3,2},{4,5},{5,4},{6,7},{7,6},{8,9},{9,8},{10,11... | collective-permute-start | bytes 135176 | tf_op jit(solution)/shard_map/ppermute | solution.py:289
  44.1 1.4 %collective-permute-done.1.b_ref = f32[8,1408]{1,0:T(8,128)S(1)} collective-permute-done((f32[8,1408]{1,0:T(8,128)S(1)}, f32[8,1408]{1,0:T(8,128)S(1)}, u32[]{:S(2)}, u32[]{:S(2)}) %collective-permute-start.1) | collective-permute-done | bytes 45088 | tf_op jit(solution)/shard_map/ppermute | solution.py:289
  45.5 0.1 pair_sum.5.a_ref
  45.6 3.0 %collective-permute-start.2 = (f32[8,1408]{1,0:T(8,128)S(1)}, f32[8,1408]{1,0:T(8,128)S(1)}, u32[]{:S(2)}, u32[]{:S(2)}) collective-permute-start(f32[8,1408]{1,0:T(8,128)S(1)} %pair_sum.5.a_ref), channel_id=1, source_target_pairs={{0,2},{1,3},{2,0},{3,1},{4,6},{5,7},{6,4},{7,5},{8,10},{9,11},{10,... | collective-permute-start | bytes 135176 | tf_op jit(solution)/shard_map/ppermute | solution.py:289
  48.6 1.4 %collective-permute-done.2.b_ref = f32[8,1408]{1,0:T(8,128)S(1)} collective-permute-done((f32[8,1408]{1,0:T(8,128)S(1)}, f32[8,1408]{1,0:T(8,128)S(1)}, u32[]{:S(2)}, u32[]{:S(2)}) %collective-permute-start.2) | collective-permute-done | bytes 45088 | tf_op jit(solution)/shard_map/ppermute | solution.py:289
  50.0 0.1 pair_sum.6.a_ref
  50.1 4.8 %collective-permute-start.3 = (f32[8,1408]{1,0:T(8,128)S(1)}, f32[8,1408]{1,0:T(8,128)S(1)}, u32[]{:S(2)}, u32[]{:S(2)}) collective-permute-start(f32[8,1408]{1,0:T(8,128)S(1)} %pair_sum.6.a_ref), channel_id=1, source_target_pairs={{0,7},{1,6},{2,5},{3,4},{4,3},{5,2},{6,1},{7,0},{8,15},{9,14},{10,... | collective-permute-start | bytes 135176 | tf_op jit(solution)/shard_map/ppermute | solution.py:289
  54.9 1.4 %collective-permute-done.3.b_ref = f32[8,1408]{1,0:T(8,128)S(1)} collective-permute-done((f32[8,1408]{1,0:T(8,128)S(1)}, f32[8,1408]{1,0:T(8,128)S(1)}, u32[]{:S(2)}, u32[]{:S(2)}) %collective-permute-start.3) | collective-permute-done | bytes 45088 | tf_op jit(solution)/shard_map/ppermute | solution.py:289
  56.4 0.1 pair_sum.7
  56.4 13.4 %all_to_all.11 = f32[16,8,1408]{2,1,0:T(8,128)S(1)} all-to-all(f32[16,8,1408]{2,1,0:T(8,128)S(1)} %pair_sum.7), channel_id=1, replica_groups=mesh['wide_0'=4,'wide_1'=4,'wide_2'=2,'narrow'=8] {'wide_0','wide_1'}, dimensions={0} | all-to-all | bytes 1441792 | tf_op jit(solution)/shard_map/all_to_all | solution.py:273
  69.8 6.1 %collective-permute-start.4 = (f32[128,1408]{1,0:T(8,128)S(1)}, f32[128,1408]{1,0:T(8,128)S(1)}, u32[]{:S(2)}, u32[]{:S(2)}) collective-permute-start(f32[128,1408]{1,0:T(8,128)S(1)} %bitcast.8), channel_id=1, source_target_pairs={{0,8},{8,0},{1,9},{9,1},{2,10},{10,2},{3,11},{11,3},{4,12},{12,4},... | collective-permute-start | bytes 2162696 | tf_op jit(solution)/shard_map/ppermute | solution.py:294
  75.9 1.8 %collective-permute-done.4.far_ref = f32[128,1408]{1,0:T(8,128)S(1)} collective-permute-done((f32[128,1408]{1,0:T(8,128)S(1)}, f32[128,1408]{1,0:T(8,128)S(1)}, u32[]{:S(2)}, u32[]{:S(2)}) %collective-permute-start.4) | collective-permute-done | bytes 720928 | tf_op jit(solution)/shard_map/ppermute | solution.py:294
  77.7 14.7 %factored.1 = (f32[256,256]{1,0:T(8,128)S(1)}, f32[256,1024]{1,0:T(8,128)}) custom-call(f32[128,1408]{1,0:T(8,128)S(1)} %bitcast.9, f32[128,1408]{1,0:T(8,128)S(1)} %collective-permute-done.4.far_ref), custom_call_target="tpu_custom_call" | custom-call | tf_op jit(solution)/shard_map/factored/pallas_call | solution.py:259
  92.4 3.1 %fusion.2 = f32[2048,256]{1,0:T(8,128)} fusion(f32[2048,256]{1,0:T(8,128)S(1)} %fusion.sample_ref, f32[256,256]{1,0:T(8,128)S(1)} %get-tuple-element.8), kind=kOutput, calls=%fused_computation.2 | convolution fusion | flops 1610612736 | bytes 4456448 | tf_op jit(solution)/shard_map/dot_general | solution.py:26
Async XLA Ops:
  0.6 1.2 %copy-start = (f32[1024,256]{1,0:T(8,128)S(1)}, f32[1024,256]{1,0:T(8,128)}, u32[]{:S(2)}) copy-start(f32[1024,256]{1,0:T(8,128)} %param.3) | copy-start | bytes 3145732
  1.9 10.0 %copy-start.1 = (f32[2048,1024]{1,0:T(8,128)S(1)}, f32[2048,1024]{1,0:T(8,128)}, u32[]{:S(2)}) copy-start(f32[2048,1024]{1,0:T(8,128)} %param.2) | copy-start | bytes 25165828
  19.5 5.1 %collective-permute-start = (f32[128,1408]{1,0:T(8,128)S(1)}, f32[128,1408]{1,0:T(8,128)S(1)}, u32[]{:S(2)}, u32[]{:S(2)}) collective-permute-start(f32[128,1408]{1,0:T(8,128)S(1)} %get-tuple-element.7), channel_id=1, source_target_pairs={{0,8},{8,0},{1,9},{9,1},{2,10},{10,2},{3,11},{11,3},{4,12},{12,4},... | collective-permute-start | bytes 2162696 | tf_op jit(solution)/shard_map/ppermute | solution.py:284
  42.2 3.3 %collective-permute-start.1 = (f32[8,1408]{1,0:T(8,128)S(1)}, f32[8,1408]{1,0:T(8,128)S(1)}, u32[]{:S(2)}, u32[]{:S(2)}) collective-permute-start(f32[8,1408]{1,0:T(8,128)S(1)} %stack_sum.1.a_ref), channel_id=1, source_target_pairs={{0,1},{1,0},{2,3},{3,2},{4,5},{5,4},{6,7},{7,6},{8,9},{9,8},{10,11... | collective-permute-start | bytes 135176 | tf_op jit(solution)/shard_map/ppermute | solution.py:289
  45.6 4.5 %collective-permute-start.2 = (f32[8,1408]{1,0:T(8,128)S(1)}, f32[8,1408]{1,0:T(8,128)S(1)}, u32[]{:S(2)}, u32[]{:S(2)}) collective-permute-start(f32[8,1408]{1,0:T(8,128)S(1)} %pair_sum.5.a_ref), channel_id=1, source_target_pairs={{0,2},{1,3},{2,0},{3,1},{4,6},{5,7},{6,4},{7,5},{8,10},{9,11},{10,... | collective-permute-start | bytes 135176 | tf_op jit(solution)/shard_map/ppermute | solution.py:289
  50.1 6.2 %collective-permute-start.3 = (f32[8,1408]{1,0:T(8,128)S(1)}, f32[8,1408]{1,0:T(8,128)S(1)}, u32[]{:S(2)}, u32[]{:S(2)}) collective-permute-start(f32[8,1408]{1,0:T(8,128)S(1)} %pair_sum.6.a_ref), channel_id=1, source_target_pairs={{0,7},{1,6},{2,5},{3,4},{4,3},{5,2},{6,1},{7,0},{8,15},{9,14},{10,... | collective-permute-start | bytes 135176 | tf_op jit(solution)/shard_map/ppermute | solution.py:289
  69.8 7.9 %collective-permute-start.4 = (f32[128,1408]{1,0:T(8,128)S(1)}, f32[128,1408]{1,0:T(8,128)S(1)}, u32[]{:S(2)}, u32[]{:S(2)}) collective-permute-start(f32[128,1408]{1,0:T(8,128)S(1)} %bitcast.8), channel_id=1, source_target_pairs={{0,8},{8,0},{1,9},{9,1},{2,10},{10,2},{3,11},{11,3},{4,12},{12,4},... | collective-permute-start | bytes 2162696 | tf_op jit(solution)/shard_map/ppermute | solution.py:294

commit v5 on v4

--- a/solution.py
+++ b/solution.py
@@ -69,7 +69,7 @@
     return [pl.BlockSpec(memory_space=pltpu.VMEM)] * n
 
 
-def gram_kernel(sample_ref, terms_ref, mine_ref, other_ref, x_ref):
+def gram_kernel(sample_ref, mine_ref, other_ref, x_ref):
     top = jnp.max(jnp.abs(sample_ref[...]), axis=0, keepdims=True)
     h, l = half_gram(sample_ref, top, 1024)
     hi, e = two_sum(h, h.T)
@@ -81,21 +81,26 @@
         x_ref[i, :, 256:320] = hi[:128, mid : mid + 64]
         x_ref[i, :, 320:] = lo[:128, mid : mid + 64]
     core = lax.axis_index(CORE)
+    mine_ref[...] = x_ref[core]
+    other_ref[...] = x_ref[1 - core]
+
+
+def halves_kernel(terms_ref, mine_ref, other_ref):
+    core = lax.axis_index(CORE)
     for half, ref in ((core, mine_ref), (1 - core, other_ref)):
-        ref[:, :GRAM] = x_ref[half]
-        ref[:, GRAM:] = terms_ref[pl.ds(pl.multiple_of(half * 128, 128), 128), :]
-
-
-def local_halves(sample, terms):
+        ref[...] = terms_ref[pl.ds(pl.multiple_of(half * 128, 128), 128), :]
+
+
+def local_halves(kernel, x, width, name, scratch, mib):
     return pl.pallas_call(
-        gram_kernel,
-        in_specs=in_vmem(2),
+        kernel,
+        in_specs=in_vmem(1),
         out_specs=in_vmem(2),
-        out_shape=[jax.ShapeDtypeStruct((128, WIDTH), F32)] * 2,
-        scratch_shapes=[pltpu.VMEM((2, 128, GRAM), F32)],
-        compiler_params=pltpu.CompilerParams(vmem_limit_bytes=20 * 2**20),
-        name="local_halves",
-    )(sample, terms)
+        out_shape=[jax.ShapeDtypeStruct((128, width), F32)] * 2,
+        scratch_shapes=scratch,
+        compiler_params=pltpu.CompilerParams(vmem_limit_bytes=mib * 2**20),
+        name=name,
+    )(x)
 
 
 def total(parts):
@@ -125,6 +130,11 @@
     for x in parts:
         ref[:, at : at + x.shape[1]] = x
         at += x.shape[1]
+
+
+def core_kernel(gram_ref, far_gram_ref, terms_ref, far_terms_ref, out_ref):
+    far = jnp.concatenate([far_gram_ref[...], far_terms_ref[...]], axis=1)
+    store(out_ref, total([jnp.concatenate([gram_ref[...], terms_ref[...]], axis=1), far]))
 
 
 def pair_kernel(a_ref, b_ref, out_ref):
@@ -218,13 +228,14 @@
     a_ref[:, :n] = g_ref[:, :n]
     a_ref[:, n:] = eye
     r_ref[...] = jnp.zeros((n, n), F32)
+    y_ref[...] = jnp.zeros((n, n), F32)
     for lo in range(0, n, BLOCK):
         hi = lo + BLOCK
-        p = dot(block_inverse(a_ref[lo:hi, lo:hi]), a_ref[lo:hi, :])
-        r_ref[lo:hi, :] = p[:, :n]
-        y_ref[lo:hi, :] = p[:, n:]
+        p = dot(block_inverse(a_ref[lo:hi, lo:hi]), a_ref[lo:hi, lo : n + hi])
+        r_ref[lo:hi, lo:] = p[:, : n - lo]
+        y_ref[lo:hi, :hi] = p[:, n - lo :]
         if hi < n:
-            a_ref[hi:, :] = a_ref[hi:, :] - dot(p[:, hi:n], p, ((0,), (0,)))
+            a_ref[hi:, hi : n + hi] = a_ref[hi:, hi : n + hi] - dot(p[:, BLOCK : n - lo], p[:, BLOCK:], ((0,), (0,)))
     r = jnp.where(row <= col, r_ref[...], 0.0)
     y = y_ref[...]
 
@@ -280,8 +291,11 @@
     swap = [(0, 1), (1, 0)]
     sample = dot(corpus, sketch)
     terms = dot(sample, corpus, ((0,), (0,)), MID)
-    mine, other = local_halves(sample, terms)
-    own = added(pair_kernel, mine.shape, "pair_sum", mine, lax.ppermute(other, CORE, swap))
+    terms, other_terms = local_halves(halves_kernel, terms, 1024, "term_halves", [], 4)
+    far_terms = lax.ppermute(other_terms, CORE, swap)
+    gram, other_gram = local_halves(gram_kernel, sample, GRAM, "gram_halves", [pltpu.VMEM((2, 128, GRAM), F32)], 20)
+    far_gram = lax.ppermute(other_gram, CORE, swap)
+    own = added(core_kernel, (128, WIDTH), "core_sum", gram, far_gram, terms, far_terms)
     whole = added(stack_kernel, (8, WIDTH), "stack_sum", exchanged(own.reshape(plane, 8, WIDTH), PLANE))
     reach = 1
     while reach < line:

time: 95.7 us -> 95.5 us (level)
    ppermute x1 -> x2, starting transfers between devices: 3.29 us -> 3.57 us  [the longest x1 3.29 us: on_device(): far_terms = lax.ppermute(other_terms, CORE, swap)]
    pallas_call x1 -> x2, Pallas kernels: 3.48 us -> 3.53 us  [local_halves(): pl.pallas_call(kernel, in_specs=in_vmem(1), out_specs=in_vmem(2), out_sha...]
  transfers between devices with their start and end apart: 5 -> 6, of which waited for: 5 -> 5; matrix products, arithmetic and copies ran while one was open for 0% -> 0% of each run, Pallas kernels for 0% -> 4%
where the time goes in v5:
time: 95.5 us; the launch traced here: 95.3 us
  blocking collectives  31 us (32%)
  starting transfers between devices  18.9 us (20%)
  Pallas kernels  18.7 us (20%)
  matrix products  17.2 us (18%)
  waiting for transfers between devices  7.56 us (8%)
  local copies, waits for them, and re-layouts  1.23 us (1%)
    all_to_all x2, blocking collectives, exchanged(): return lax.all_to_all(x, axis, 0, 0, tiled=True)  31 us
    dot_general x3, matrix products, dot(): lax.dot_general(a, b, (dims, ((), ())), precision=precision, preferred_el...  17.2 us
    pallas_call x1, Pallas kernels, factored(): pl.pallas_call(functools.partial(factor_kernel, root), in_specs=in_vmem(2...  14.7 us
    ppermute x3, starting transfers between devices, on_device(): arrived = lax.ppermute(whole, LINE, [(i, i ^ flip) for i in range(line)])  9.5 us
    ppermute x1, starting transfers between devices, on_device(): far = lax.ppermute(near, CORE, swap)  5.84 us
    ppermute x3, waiting for transfers between devices, on_device(): arrived = lax.ppermute(whole, LINE, [(i, i ^ flip) for i in range(line)])  4.32 us
    pallas_call x2, Pallas kernels, local_halves(): pl.pallas_call(kernel, in_specs=in_vmem(1), out_specs=in_vmem(2), out_sha...  3.53 us
    ppermute x1, starting transfers between devices, on_device(): far_terms = lax.ppermute(other_terms, CORE, swap)  3.29 us
  transfers between devices with their start and end apart: 6, of which 5 were waited for; matrix products, arithmetic and copies ran while one was open for 0% of the time, Pallas kernels for 4%

profile of v5, /device:TPU:1, one launch (start us, length us, event | category | flops | bytes accessed | tf_op | source)
XLA Modules:
  0.0 95.3 jit_solution(7509207538591035862)
XLA Ops:
  0.6 0.0 copy-start
  0.6 1.2 %copy-done = f32[1024,256]{1,0:T(8,128)S(1)} copy-done((f32[1024,256]{1,0:T(8,128)S(1)}, f32[1024,256]{1,0:T(8,128)}, u32[]{:S(2)}) %copy-start) | copy-done | bytes 1048600
  1.9 0.0 copy-start.1
  1.9 9.9 %fusion.sample_ref = f32[2048,256]{1,0:T(8,128)S(1)} fusion(f32[2048,1024]{1,0:T(8,128)} %param.2, f32[1024,256]{1,0:T(8,128)S(1)} %copy-done), kind=kOutput, calls=%fused_computation | convolution fusion | flops 6442450944 | bytes 11534336 | tf_op jit(solution)/shard_map/dot_general | solution.py:26
  11.8 0.0 copy-done.1
  11.8 4.2 %fusion.1.terms_ref = f32[256,1024]{1,0:T(8,128)S(1)} fusion(f32[2048,256]{1,0:T(8,128)S(1)} %fusion.sample_ref, f32[2048,1024]{1,0:T(8,128)S(1)} %copy-done.1), kind=kOutput, calls=%fused_computation.1 | convolution fusion | flops 3221225472 | bytes 11534336 | tf_op jit(solution)/shard_map/dot_general | solution.py:26
  16.0 0.1 term_halves.1
  16.1 3.3 %collective-permute-start.1 = (f32[128,1024]{1,0:T(8,128)S(1)}, f32[128,1024]{1,0:T(8,128)S(1)}, u32[]{:S(2)}, u32[]{:S(2)}) collective-permute-start(f32[128,1024]{1,0:T(8,128)S(1)} %get-tuple-element.11), channel_id=1, source_target_pairs={{0,8},{8,0},{1,9},{9,1},{2,10},{10,2},{3,11},{11,3},{4,12},{12,4},... | collective-permute-start | bytes 1572872 | tf_op jit(solution)/shard_map/ppermute | solution.py:295
  19.4 3.5 %gram_halves.1 = (f32[128,384]{1,0:T(8,128)S(1)}, f32[128,384]{1,0:T(8,128)S(1)}) custom-call(f32[2048,256]{1,0:T(8,128)S(1)} %fusion.sample_ref), custom_call_target="tpu_custom_call" | custom-call | tf_op jit(solution)/shard_map/gram_halves/pallas_call | solution.py:95
  22.8 0.3 collective-permute-start
  23.1 1.4 %collective-permute-done.far_gram_ref = f32[128,384]{1,0:T(8,128)S(1)} collective-permute-done((f32[128,384]{1,0:T(8,128)S(1)}, f32[128,384]{1,0:T(8,128)S(1)}, u32[]{:S(2)}, u32[]{:S(2)}) %collective-permute-start) | collective-permute-done | bytes 196640 | tf_op jit(solution)/shard_map/ppermute | solution.py:297
  24.5 0.0 collective-permute-done.1.far_terms_ref
  24.5 0.1 core_sum.1
  24.6 17.6 %all_to_all.10.x_ref = f32[16,8,1408]{2,1,0:T(8,128)S(1)} all-to-all(f32[16,8,1408]{2,1,0:T(8,128)S(1)} %bitcast.10), channel_id=1, replica_groups=mesh['wide_0'=4,'wide_1'=4,'wide_2'=2,'narrow'=8] {'wide_0','wide_1'}, dimensions={0} | all-to-all | bytes 1441792 | tf_op jit(solution)/shard_map/all_to_all | solution.py:284
  42.2 0.1 stack_sum.1.a_ref
  42.3 1.7 %collective-permute-start.2 = (f32[8,1408]{1,0:T(8,128)S(1)}, f32[8,1408]{1,0:T(8,128)S(1)}, u32[]{:S(2)}, u32[]{:S(2)}) collective-permute-start(f32[8,1408]{1,0:T(8,128)S(1)} %stack_sum.1.a_ref), channel_id=1, source_target_pairs={{0,1},{1,0},{2,3},{3,2},{4,5},{5,4},{6,7},{7,6},{8,9},{9,8},{10,11... | collective-permute-start | bytes 135176 | tf_op jit(solution)/shard_map/ppermute | solution.py:303
  44.0 1.4 %collective-permute-done.2.b_ref = f32[8,1408]{1,0:T(8,128)S(1)} collective-permute-done((f32[8,1408]{1,0:T(8,128)S(1)}, f32[8,1408]{1,0:T(8,128)S(1)}, u32[]{:S(2)}, u32[]{:S(2)}) %collective-permute-start.2) | collective-permute-done | bytes 45088 | tf_op jit(solution)/shard_map/ppermute | solution.py:303
  45.5 0.1 pair_sum.3.a_ref
  45.5 3.0 %collective-permute-start.3 = (f32[8,1408]{1,0:T(8,128)S(1)}, f32[8,1408]{1,0:T(8,128)S(1)}, u32[]{:S(2)}, u32[]{:S(2)}) collective-permute-start(f32[8,1408]{1,0:T(8,128)S(1)} %pair_sum.3.a_ref), channel_id=1, source_target_pairs={{0,2},{1,3},{2,0},{3,1},{4,6},{5,7},{6,4},{7,5},{8,10},{9,11},{10,... | collective-permute-start | bytes 135176 | tf_op jit(solution)/shard_map/ppermute | solution.py:303
  48.6 1.4 %collective-permute-done.3.b_ref = f32[8,1408]{1,0:T(8,128)S(1)} collective-permute-done((f32[8,1408]{1,0:T(8,128)S(1)}, f32[8,1408]{1,0:T(8,128)S(1)}, u32[]{:S(2)}, u32[]{:S(2)}) %collective-permute-start.3) | collective-permute-done | bytes 45088 | tf_op jit(solution)/shard_map/ppermute | solution.py:303
  50.0 0.1 pair_sum.4.a_ref
  50.1 4.8 %collective-permute-start.4 = (f32[8,1408]{1,0:T(8,128)S(1)}, f32[8,1408]{1,0:T(8,128)S(1)}, u32[]{:S(2)}, u32[]{:S(2)}) collective-permute-start(f32[8,1408]{1,0:T(8,128)S(1)} %pair_sum.4.a_ref), channel_id=1, source_target_pairs={{0,7},{1,6},{2,5},{3,4},{4,3},{5,2},{6,1},{7,0},{8,15},{9,14},{10,... | collective-permute-start | bytes 135176 | tf_op jit(solution)/shard_map/ppermute | solution.py:303
  54.9 1.4 %collective-permute-done.4.b_ref = f32[8,1408]{1,0:T(8,128)S(1)} collective-permute-done((f32[8,1408]{1,0:T(8,128)S(1)}, f32[8,1408]{1,0:T(8,128)S(1)}, u32[]{:S(2)}, u32[]{:S(2)}) %collective-permute-start.4) | collective-permute-done | bytes 45088 | tf_op jit(solution)/shard_map/ppermute | solution.py:303
  56.3 0.1 pair_sum.5
  56.4 13.4 %all_to_all.11 = f32[16,8,1408]{2,1,0:T(8,128)S(1)} all-to-all(f32[16,8,1408]{2,1,0:T(8,128)S(1)} %pair_sum.5), channel_id=1, replica_groups=mesh['wide_0'=4,'wide_1'=4,'wide_2'=2,'narrow'=8] {'wide_0','wide_1'}, dimensions={0} | all-to-all | bytes 1441792 | tf_op jit(solution)/shard_map/all_to_all | solution.py:284
  69.8 5.8 %collective-permute-start.5 = (f32[128,1408]{1,0:T(8,128)S(1)}, f32[128,1408]{1,0:T(8,128)S(1)}, u32[]{:S(2)}, u32[]{:S(2)}) collective-permute-start(f32[128,1408]{1,0:T(8,128)S(1)} %bitcast.8), channel_id=1, source_target_pairs={{0,8},{8,0},{1,9},{9,1},{2,10},{10,2},{3,11},{11,3},{4,12},{12,4},... | collective-permute-start | bytes 2162696 | tf_op jit(solution)/shard_map/ppermute | solution.py:308
  75.6 1.8 %collective-permute-done.5.far_ref = f32[128,1408]{1,0:T(8,128)S(1)} collective-permute-done((f32[128,1408]{1,0:T(8,128)S(1)}, f32[128,1408]{1,0:T(8,128)S(1)}, u32[]{:S(2)}, u32[]{:S(2)}) %collective-permute-start.5) | collective-permute-done | bytes 720928 | tf_op jit(solution)/shard_map/ppermute | solution.py:308
  77.4 14.7 %factored.1 = (f32[256,256]{1,0:T(8,128)S(1)}, f32[256,1024]{1,0:T(8,128)}) custom-call(f32[128,1408]{1,0:T(8,128)S(1)} %bitcast.9, f32[128,1408]{1,0:T(8,128)S(1)} %collective-permute-done.5.far_ref), custom_call_target="tpu_custom_call" | custom-call | tf_op jit(solution)/shard_map/factored/pallas_call | solution.py:270
  92.2 3.1 %fusion.2 = f32[2048,256]{1,0:T(8,128)} fusion(f32[2048,256]{1,0:T(8,128)S(1)} %fusion.sample_ref, f32[256,256]{1,0:T(8,128)S(1)} %get-tuple-element.12), kind=kOutput, calls=%fused_computation.2 | convolution fusion | flops 1610612736 | bytes 4456448 | tf_op jit(solution)/shard_map/dot_general | solution.py:26
Async XLA Ops:
  0.6 1.2 %copy-start = (f32[1024,256]{1,0:T(8,128)S(1)}, f32[1024,256]{1,0:T(8,128)}, u32[]{:S(2)}) copy-start(f32[1024,256]{1,0:T(8,128)} %param.3) | copy-start | bytes 3145732
  1.9 10.0 %copy-start.1 = (f32[2048,1024]{1,0:T(8,128)S(1)}, f32[2048,1024]{1,0:T(8,128)}, u32[]{:S(2)}) copy-start(f32[2048,1024]{1,0:T(8,128)} %param.2) | copy-start | bytes 25165828
  16.1 8.5 %collective-permute-start.1 = (f32[128,1024]{1,0:T(8,128)S(1)}, f32[128,1024]{1,0:T(8,128)S(1)}, u32[]{:S(2)}, u32[]{:S(2)}) collective-permute-start(f32[128,1024]{1,0:T(8,128)S(1)} %get-tuple-element.11), channel_id=1, source_target_pairs={{0,8},{8,0},{1,9},{9,1},{2,10},{10,2},{3,11},{11,3},{4,12},{12,4},... | collective-permute-start | bytes 1572872 | tf_op jit(solution)/shard_map/ppermute | solution.py:295
  22.8 1.7 %collective-permute-start = (f32[128,384]{1,0:T(8,128)S(1)}, f32[128,384]{1,0:T(8,128)S(1)}, u32[]{:S(2)}, u32[]{:S(2)}) collective-permute-start(f32[128,384]{1,0:T(8,128)S(1)} %get-tuple-element.9), channel_id=1, source_target_pairs={{0,8},{8,0},{1,9},{9,1},{2,10},{10,2},{3,11},{11,3},{4,12},{12,4},... | collective-permute-start | bytes 589832 | tf_op jit(solution)/shard_map/ppermute | solution.py:297
  42.3 3.1 %collective-permute-start.2 = (f32[8,1408]{1,0:T(8,128)S(1)}, f32[8,1408]{1,0:T(8,128)S(1)}, u32[]{:S(2)}, u32[]{:S(2)}) collective-permute-start(f32[8,1408]{1,0:T(8,128)S(1)} %stack_sum.1.a_ref), channel_id=1, source_target_pairs={{0,1},{1,0},{2,3},{3,2},{4,5},{5,4},{6,7},{7,6},{8,9},{9,8},{10,11... | collective-permute-start | bytes 135176 | tf_op jit(solution)/shard_map/ppermute | solution.py:303
  45.5 4.5 %collective-permute-start.3 = (f32[8,1408]{1,0:T(8,128)S(1)}, f32[8,1408]{1,0:T(8,128)S(1)}, u32[]{:S(2)}, u32[]{:S(2)}) collective-permute-start(f32[8,1408]{1,0:T(8,128)S(1)} %pair_sum.3.a_ref), channel_id=1, source_target_pairs={{0,2},{1,3},{2,0},{3,1},{4,6},{5,7},{6,4},{7,5},{8,10},{9,11},{10,... | collective-permute-start | bytes 135176 | tf_op jit(solution)/shard_map/ppermute | solution.py:303
  50.1 6.2 %collective-permute-start.4 = (f32[8,1408]{1,0:T(8,128)S(1)}, f32[8,1408]{1,0:T(8,128)S(1)}, u32[]{:S(2)}, u32[]{:S(2)}) collective-permute-start(f32[8,1408]{1,0:T(8,128)S(1)} %pair_sum.4.a_ref), channel_id=1, source_target_pairs={{0,7},{1,6},{2,5},{3,4},{4,3},{5,2},{6,1},{7,0},{8,15},{9,14},{10,... | collective-permute-start | bytes 135176 | tf_op jit(solution)/shard_map/ppermute | solution.py:303
  69.8 7.7 %collective-permute-start.5 = (f32[128,1408]{1,0:T(8,128)S(1)}, f32[128,1408]{1,0:T(8,128)S(1)}, u32[]{:S(2)}, u32[]{:S(2)}) collective-permute-start(f32[128,1408]{1,0:T(8,128)S(1)} %bitcast.8), channel_id=1, source_target_pairs={{0,8},{8,0},{1,9},{9,1},{2,10},{10,2},{3,11},{11,3},{4,12},{12,4},... | collective-permute-start | bytes 2162696 | tf_op jit(solution)/shard_map/ppermute | solution.py:308

commit v6 on v5

--- a/solution.py
+++ b/solution.py
@@ -228,14 +228,13 @@
     a_ref[:, :n] = g_ref[:, :n]
     a_ref[:, n:] = eye
     r_ref[...] = jnp.zeros((n, n), F32)
-    y_ref[...] = jnp.zeros((n, n), F32)
     for lo in range(0, n, BLOCK):
         hi = lo + BLOCK
-        p = dot(block_inverse(a_ref[lo:hi, lo:hi]), a_ref[lo:hi, lo : n + hi])
-        r_ref[lo:hi, lo:] = p[:, : n - lo]
-        y_ref[lo:hi, :hi] = p[:, n - lo :]
+        p = dot(block_inverse(a_ref[lo:hi, lo:hi]), a_ref[lo:hi, :])
+        r_ref[lo:hi, :] = p[:, :n]
+        y_ref[lo:hi, :] = p[:, n:]
         if hi < n:
-            a_ref[hi:, hi : n + hi] = a_ref[hi:, hi : n + hi] - dot(p[:, BLOCK : n - lo], p[:, BLOCK:], ((0,), (0,)))
+            a_ref[hi:, :] = a_ref[hi:, :] - dot(p[:, hi:n], p, ((0,), (0,)))
     r = jnp.where(row <= col, r_ref[...], 0.0)
     y = y_ref[...]
 
@@ -248,19 +247,22 @@
     d = d + ((g_ref[:, n:] - fine) + (e1 + e2))
 
     f = dot(r, y, nt) - eye
-    m = eye + ((f + f.T) + dot(f, f, tn, MID) + dot(dot(y, d, precision=MID), y, nt, MID))
+    m = (f + f.T) + dot(f, f, tn, MID) + dot(dot(y, d, precision=MID), y, nt, MID)
     m_ref[...] = m
-    u_ref[...] = eye - lower * (m - eye)
+    u_ref[...] = lower * m
 
     def refine(carry):
         count, _ = carry
-        u = u_ref[...]
-        off = dot(dot(u, m_ref[...]), u, nt) - eye
-        u_ref[...] = u - dot(lower * off, u, precision=MID)
+        u, m = u_ref[...], m_ref[...]
+        um = dot(u, m, precision=MID)
+        once = u + um
+        off = ((m - once) - once.T) + (dot(u, u, nt, MID) + dot(um, u, nt, MID))
+        step = lower * off
+        u_ref[...] = u + (step - dot(step, u, precision=MID))
         return count + 1, jnp.max(jnp.abs(off))
 
     lax.while_loop(lambda c: (c[0] < 24) & (c[1] > 1e-4), refine, (0, jnp.float32(1.0)))
-    y = dot(u_ref[...], y)
+    y = y - dot(u_ref[...], y)
     inverse_ref[...] = (y * root).T
     projection_ref[...] = dot(y * (1.0 / root), w_ref[...])
 

time: 95.5 us -> 95.4 us (level)
  no operation moved by 1% of the time
where the time goes in v6:
time: 95.4 us; the launch traced here: 95.2 us
  blocking collectives  31 us (32%)
  starting transfers between devices  18.9 us (20%)
  Pallas kernels  18.6 us (19%)
  matrix products  17.2 us (18%)
  waiting for transfers between devices  7.56 us (8%)
  local copies, waits for them, and re-layouts  1.23 us (1%)
    all_to_all x2, blocking collectives, exchanged(): return lax.all_to_all(x, axis, 0, 0, tiled=True)  31 us
    dot_general x3, matrix products, dot(): lax.dot_general(a, b, (dims, ((), ())), precision=precision, preferred_el...  17.2 us
    pallas_call x1, Pallas kernels, factored(): pl.pallas_call(functools.partial(factor_kernel, root), in_specs=in_vmem(2...  14.6 us
    ppermute x3, starting transfers between devices, on_device(): arrived = lax.ppermute(whole, LINE, [(i, i ^ flip) for i in range(line)])  9.5 us
    ppermute x1, starting transfers between devices, on_device(): far = lax.ppermute(near, CORE, swap)  5.84 us
    ppermute x3, waiting for transfers between devices, on_device(): arrived = lax.ppermute(whole, LINE, [(i, i ^ flip) for i in range(line)])  4.32 us
    pallas_call x2, Pallas kernels, local_halves(): pl.pallas_call(kernel, in_specs=in_vmem(1), out_specs=in_vmem(2), out_sha...  3.53 us
    ppermute x1, starting transfers between devices, on_device(): far_terms = lax.ppermute(other_terms, CORE, swap)  3.29 us
  transfers between devices with their start and end apart: 6, of which 5 were waited for; matrix products, arithmetic and copies ran while one was open for 0% of the time, Pallas kernels for 4%

profile of v6, /device:TPU:1, one launch (start us, length us, event | category | flops | bytes accessed | tf_op | source)
XLA Modules:
  0.0 95.2 jit_solution(3749919825229140215)
XLA Ops:
  0.6 0.0 copy-start
  0.6 1.2 %copy-done = f32[1024,256]{1,0:T(8,128)S(1)} copy-done((f32[1024,256]{1,0:T(8,128)S(1)}, f32[1024,256]{1,0:T(8,128)}, u32[]{:S(2)}) %copy-start) | copy-done | bytes 1048600
  1.9 0.0 copy-start.1
  1.9 9.9 %fusion.sample_ref = f32[2048,256]{1,0:T(8,128)S(1)} fusion(f32[2048,1024]{1,0:T(8,128)} %param.2, f32[1024,256]{1,0:T(8,128)S(1)} %copy-done), kind=kOutput, calls=%fused_computation | convolution fusion | flops 6442450944 | bytes 11534336 | tf_op jit(solution)/shard_map/dot_general | solution.py:26
  11.8 0.0 copy-done.1
  11.8 4.2 %fusion.1.terms_ref = f32[256,1024]{1,0:T(8,128)S(1)} fusion(f32[2048,256]{1,0:T(8,128)S(1)} %fusion.sample_ref, f32[2048,1024]{1,0:T(8,128)S(1)} %copy-done.1), kind=kOutput, calls=%fused_computation.1 | convolution fusion | flops 3221225472 | bytes 11534336 | tf_op jit(solution)/shard_map/dot_general | solution.py:26
  16.0 0.1 term_halves.1
  16.1 3.3 %collective-permute-start.1 = (f32[128,1024]{1,0:T(8,128)S(1)}, f32[128,1024]{1,0:T(8,128)S(1)}, u32[]{:S(2)}, u32[]{:S(2)}) collective-permute-start(f32[128,1024]{1,0:T(8,128)S(1)} %get-tuple-element.11), channel_id=1, source_target_pairs={{0,8},{8,0},{1,9},{9,1},{2,10},{10,2},{3,11},{11,3},{4,12},{12,4},... | collective-permute-start | bytes 1572872 | tf_op jit(solution)/shard_map/ppermute | solution.py:297
  19.4 3.5 %gram_halves.1 = (f32[128,384]{1,0:T(8,128)S(1)}, f32[128,384]{1,0:T(8,128)S(1)}) custom-call(f32[2048,256]{1,0:T(8,128)S(1)} %fusion.sample_ref), custom_call_target="tpu_custom_call" | custom-call | tf_op jit(solution)/shard_map/gram_halves/pallas_call | solution.py:95
  22.8 0.3 collective-permute-start
  23.1 1.4 %collective-permute-done.far_gram_ref = f32[128,384]{1,0:T(8,128)S(1)} collective-permute-done((f32[128,384]{1,0:T(8,128)S(1)}, f32[128,384]{1,0:T(8,128)S(1)}, u32[]{:S(2)}, u32[]{:S(2)}) %collective-permute-start) | collective-permute-done | bytes 196640 | tf_op jit(solution)/shard_map/ppermute | solution.py:299
  24.5 0.0 collective-permute-done.1.far_terms_ref
  24.5 0.1 core_sum.1
  24.6 17.6 %all_to_all.10.x_ref = f32[16,8,1408]{2,1,0:T(8,128)S(1)} all-to-all(f32[16,8,1408]{2,1,0:T(8,128)S(1)} %bitcast.10), channel_id=1, replica_groups=mesh['wide_0'=4,'wide_1'=4,'wide_2'=2,'narrow'=8] {'wide_0','wide_1'}, dimensions={0} | all-to-all | bytes 1441792 | tf_op jit(solution)/shard_map/all_to_all | solution.py:286
  42.2 0.1 stack_sum.1.a_ref
  42.3 1.7 %collective-permute-start.2 = (f32[8,1408]{1,0:T(8,128)S(1)}, f32[8,1408]{1,0:T(8,128)S(1)}, u32[]{:S(2)}, u32[]{:S(2)}) collective-permute-start(f32[8,1408]{1,0:T(8,128)S(1)} %stack_sum.1.a_ref), channel_id=1, source_target_pairs={{0,1},{1,0},{2,3},{3,2},{4,5},{5,4},{6,7},{7,6},{8,9},{9,8},{10,11... | collective-permute-start | bytes 135176 | tf_op jit(solution)/shard_map/ppermute | solution.py:305
  44.0 1.4 %collective-permute-done.2.b_ref = f32[8,1408]{1,0:T(8,128)S(1)} collective-permute-done((f32[8,1408]{1,0:T(8,128)S(1)}, f32[8,1408]{1,0:T(8,128)S(1)}, u32[]{:S(2)}, u32[]{:S(2)}) %collective-permute-start.2) | collective-permute-done | bytes 45088 | tf_op jit(solution)/shard_map/ppermute | solution.py:305
  45.5 0.1 pair_sum.3.a_ref
  45.5 3.0 %collective-permute-start.3 = (f32[8,1408]{1,0:T(8,128)S(1)}, f32[8,1408]{1,0:T(8,128)S(1)}, u32[]{:S(2)}, u32[]{:S(2)}) collective-permute-start(f32[8,1408]{1,0:T(8,128)S(1)} %pair_sum.3.a_ref), channel_id=1, source_target_pairs={{0,2},{1,3},{2,0},{3,1},{4,6},{5,7},{6,4},{7,5},{8,10},{9,11},{10,... | collective-permute-start | bytes 135176 | tf_op jit(solution)/shard_map/ppermute | solution.py:305
  48.6 1.4 %collective-permute-done.3.b_ref = f32[8,1408]{1,0:T(8,128)S(1)} collective-permute-done((f32[8,1408]{1,0:T(8,128)S(1)}, f32[8,1408]{1,0:T(8,128)S(1)}, u32[]{:S(2)}, u32[]{:S(2)}) %collective-permute-start.3) | collective-permute-done | bytes 45088 | tf_op jit(solution)/shard_map/ppermute | solution.py:305
  50.0 0.1 pair_sum.4.a_ref
  50.1 4.8 %collective-permute-start.4 = (f32[8,1408]{1,0:T(8,128)S(1)}, f32[8,1408]{1,0:T(8,128)S(1)}, u32[]{:S(2)}, u32[]{:S(2)}) collective-permute-start(f32[8,1408]{1,0:T(8,128)S(1)} %pair_sum.4.a_ref), channel_id=1, source_target_pairs={{0,7},{1,6},{2,5},{3,4},{4,3},{5,2},{6,1},{7,0},{8,15},{9,14},{10,... | collective-permute-start | bytes 135176 | tf_op jit(solution)/shard_map/ppermute | solution.py:305
  54.9 1.4 %collective-permute-done.4.b_ref = f32[8,1408]{1,0:T(8,128)S(1)} collective-permute-done((f32[8,1408]{1,0:T(8,128)S(1)}, f32[8,1408]{1,0:T(8,128)S(1)}, u32[]{:S(2)}, u32[]{:S(2)}) %collective-permute-start.4) | collective-permute-done | bytes 45088 | tf_op jit(solution)/shard_map/ppermute | solution.py:305
  56.3 0.1 pair_sum.5
  56.4 13.4 %all_to_all.11 = f32[16,8,1408]{2,1,0:T(8,128)S(1)} all-to-all(f32[16,8,1408]{2,1,0:T(8,128)S(1)} %pair_sum.5), channel_id=1, replica_groups=mesh['wide_0'=4,'wide_1'=4,'wide_2'=2,'narrow'=8] {'wide_0','wide_1'}, dimensions={0} | all-to-all | bytes 1441792 | tf_op jit(solution)/shard_map/all_to_all | solution.py:286
  69.8 5.8 %collective-permute-start.5 = (f32[128,1408]{1,0:T(8,128)S(1)}, f32[128,1408]{1,0:T(8,128)S(1)}, u32[]{:S(2)}, u32[]{:S(2)}) collective-permute-start(f32[128,1408]{1,0:T(8,128)S(1)} %bitcast.8), channel_id=1, source_target_pairs={{0,8},{8,0},{1,9},{9,1},{2,10},{10,2},{3,11},{11,3},{4,12},{12,4},... | collective-permute-start | bytes 2162696 | tf_op jit(solution)/shard_map/ppermute | solution.py:310
  75.6 1.8 %collective-permute-done.5.far_ref = f32[128,1408]{1,0:T(8,128)S(1)} collective-permute-done((f32[128,1408]{1,0:T(8,128)S(1)}, f32[128,1408]{1,0:T(8,128)S(1)}, u32[]{:S(2)}, u32[]{:S(2)}) %collective-permute-start.5) | collective-permute-done | bytes 720928 | tf_op jit(solution)/shard_map/ppermute | solution.py:310
  77.4 14.6 %factored.1 = (f32[256,256]{1,0:T(8,128)S(1)}, f32[256,1024]{1,0:T(8,128)}) custom-call(f32[128,1408]{1,0:T(8,128)S(1)} %bitcast.9, f32[128,1408]{1,0:T(8,128)S(1)} %collective-permute-done.5.far_ref), custom_call_target="tpu_custom_call" | custom-call | tf_op jit(solution)/shard_map/factored/pallas_call | solution.py:272
  92.0 3.1 %fusion.2 = f32[2048,256]{1,0:T(8,128)} fusion(f32[2048,256]{1,0:T(8,128)S(1)} %fusion.sample_ref, f32[256,256]{1,0:T(8,128)S(1)} %get-tuple-element.12), kind=kOutput, calls=%fused_computation.2 | convolution fusion | flops 1610612736 | bytes 4456448 | tf_op jit(solution)/shard_map/dot_general | solution.py:26
Async XLA Ops:
  0.6 1.2 %copy-start = (f32[1024,256]{1,0:T(8,128)S(1)}, f32[1024,256]{1,0:T(8,128)}, u32[]{:S(2)}) copy-start(f32[1024,256]{1,0:T(8,128)} %param.3) | copy-start | bytes 3145732
  1.9 10.0 %copy-start.1 = (f32[2048,1024]{1,0:T(8,128)S(1)}, f32[2048,1024]{1,0:T(8,128)}, u32[]{:S(2)}) copy-start(f32[2048,1024]{1,0:T(8,128)} %param.2) | copy-start | bytes 25165828
  16.1 8.5 %collective-permute-start.1 = (f32[128,1024]{1,0:T(8,128)S(1)}, f32[128,1024]{1,0:T(8,128)S(1)}, u32[]{:S(2)}, u32[]{:S(2)}) collective-permute-start(f32[128,1024]{1,0:T(8,128)S(1)} %get-tuple-element.11), channel_id=1, source_target_pairs={{0,8},{8,0},{1,9},{9,1},{2,10},{10,2},{3,11},{11,3},{4,12},{12,4},... | collective-permute-start | bytes 1572872 | tf_op jit(solution)/shard_map/ppermute | solution.py:297
  22.8 1.7 %collective-permute-start = (f32[128,384]{1,0:T(8,128)S(1)}, f32[128,384]{1,0:T(8,128)S(1)}, u32[]{:S(2)}, u32[]{:S(2)}) collective-permute-start(f32[128,384]{1,0:T(8,128)S(1)} %get-tuple-element.9), channel_id=1, source_target_pairs={{0,8},{8,0},{1,9},{9,1},{2,10},{10,2},{3,11},{11,3},{4,12},{12,4},... | collective-permute-start | bytes 589832 | tf_op jit(solution)/shard_map/ppermute | solution.py:299
  42.3 3.1 %collective-permute-start.2 = (f32[8,1408]{1,0:T(8,128)S(1)}, f32[8,1408]{1,0:T(8,128)S(1)}, u32[]{:S(2)}, u32[]{:S(2)}) collective-permute-start(f32[8,1408]{1,0:T(8,128)S(1)} %stack_sum.1.a_ref), channel_id=1, source_target_pairs={{0,1},{1,0},{2,3},{3,2},{4,5},{5,4},{6,7},{7,6},{8,9},{9,8},{10,11... | collective-permute-start | bytes 135176 | tf_op jit(solution)/shard_map/ppermute | solution.py:305
  45.5 4.5 %collective-permute-start.3 = (f32[8,1408]{1,0:T(8,128)S(1)}, f32[8,1408]{1,0:T(8,128)S(1)}, u32[]{:S(2)}, u32[]{:S(2)}) collective-permute-start(f32[8,1408]{1,0:T(8,128)S(1)} %pair_sum.3.a_ref), channel_id=1, source_target_pairs={{0,2},{1,3},{2,0},{3,1},{4,6},{5,7},{6,4},{7,5},{8,10},{9,11},{10,... | collective-permute-start | bytes 135176 | tf_op jit(solution)/shard_map/ppermute | solution.py:305
  50.1 6.2 %collective-permute-start.4 = (f32[8,1408]{1,0:T(8,128)S(1)}, f32[8,1408]{1,0:T(8,128)S(1)}, u32[]{:S(2)}, u32[]{:S(2)}) collective-permute-start(f32[8,1408]{1,0:T(8,128)S(1)} %pair_sum.4.a_ref), channel_id=1, source_target_pairs={{0,7},{1,6},{2,5},{3,4},{4,3},{5,2},{6,1},{7,0},{8,15},{9,14},{10,... | collective-permute-start | bytes 135176 | tf_op jit(solution)/shard_map/ppermute | solution.py:305
  69.8 7.7 %collective-permute-start.5 = (f32[128,1408]{1,0:T(8,128)S(1)}, f32[128,1408]{1,0:T(8,128)S(1)}, u32[]{:S(2)}, u32[]{:S(2)}) collective-permute-start(f32[128,1408]{1,0:T(8,128)S(1)} %bitcast.8), channel_id=1, source_target_pairs={{0,8},{8,0},{1,9},{9,1},{2,10},{10,2},{3,11},{11,3},{4,12},{12,4},... | collective-permute-start | bytes 2162696 | tf_op jit(solution)/shard_map/ppermute | solution.py:310
